TPU v7x, 512 devices: a whole 4x8x8 slice. The times are simulated.
512 devices in a mesh: segment: 8 (over x, core), adapter: 64 (over z, y).
Axes of the slice: x: 4, y: 8, z: 8, core: 2. Of those that a mesh axis runs over, the one named last changes fastest.
Arguments:
- incoming: bfloat16 [4096, 8192], P(('segment', 'adapter')), may hold values from -6 to 6
- attention_norm_gain: float32 [8, 8192], P('segment'), may hold values from 0.1 to 1.9
- query_weight: bfloat16 [8, 8192, 8192], P('segment', None, 'adapter'), may hold values from -0.0625 to 0.0625
- adapter_down_weight: bfloat16 [8, 64, 8192, 64], P('segment', 'adapter'), may hold values from -0.0625 to 0.0625
- adapter_up_weight: bfloat16 [8, 64, 64, 8192], P('segment', None, None, 'adapter'), may hold values from -0.75 to 0.75
- request_adapter_index: int32 [4096], P('segment'), may hold values from 0 to 63, as said below
- cache_valid_length: int32 [4096], P('segment'), may hold values from 1 to 16
- key_value_cache: bfloat16 [4096, 2, 16, 1024], P(('segment', 'adapter')), may hold values from -1500 to 1500, as said below
Outputs:
- context: bfloat16 [4096, 8192], P(('segment', 'adapter'))
Inputs may be any that keep to these rules, and one draw needn't show every extreme that they name: `request_adapter_index`: adapter a is owned by index a // 1 of adapter. At most 32 of the 512 requests of one section name adapters of one owner, and in every section some owner has exactly 32. `key_value_cache`: positions at or after a request's length hold unused entries.
All inputs are finite; a program needn't handle non-finite values.
Results may differ from a plain program's by a relative error of at most 0.04.
Values may be sent and summed in bfloat16 or wider, within the bound.
No kernel may reach another device: no remote copies, remote signals or barrier semaphores. Data moves between devices by JAX's collectives and lax.ppermute only.
A program may use at most 64 MiB of HBM per device.

v0:
```python
import jax
import jax.numpy as jnp
from jax import lax
from jax.sharding import PartitionSpec as P

MODEL_WIDTH = 8192
HEADS = 64
KVH = 8
HD = 128
CTX = 16


adapter_scale = 0.5
norm_eps = 1e-05


def from_behind(value, axis, by):
    devices = lax.axis_size(axis)
    return lax.ppermute(value, axis, [(i, (i + by) % devices) for i in range(devices)])


def body(
    incoming,
    attention_norm_gain,
    query_weight,
    adapter_down_weight,
    adapter_up_weight,
    request_adapter_index,
    cache_valid_length,
    key_value_cache,
):
    received_rows = from_behind(incoming, "segment", 1)
    values = received_rows.astype(jnp.float32)
    mean_square = jnp.mean(values * values, axis=-1, keepdims=True)
    normalized_input = (values * lax.rsqrt(mean_square + norm_eps) * attention_norm_gain[0]).astype(
        jnp.bfloat16
    )
    tok_dev = received_rows.shape[0]
    position = lax.axis_index("adapter")
    segment_rows = request_adapter_index.shape[0]
    weight = query_weight[0]
    column_list = weight.shape[1]
    down_matrices = adapter_down_weight[0]
    ad_dev = down_matrices.shape[0]
    adapter_rank_width = down_matrices.shape[2]
    adapter_bank = adapter_up_weight.shape[1]
    owner_of = request_adapter_index // ad_dev
    local_of = request_adapter_index % ad_dev
    row_piece = lax.all_gather(normalized_input, "adapter", axis=0, tiled=True)
    plain = jnp.dot(row_piece, weight, preferred_element_type=jnp.float32)
    shrunk = jnp.einsum("td,adr->tar", row_piece, down_matrices, preferred_element_type=jnp.float32)
    projected = jnp.concatenate(
        [plain, shrunk.reshape(row_piece.shape[0], ad_dev * adapter_rank_width)], axis=1
    )
    base_query = projected[:, :column_list]
    shrunk_all = projected[:, column_list:].reshape(segment_rows, ad_dev, adapter_rank_width)
    select_mask = (local_of[:, None] == jnp.arange(ad_dev, dtype=jnp.int32)[None, :]) & (
        owner_of == position
    )[:, None]
    shrunk_mine = jnp.sum(shrunk_all * select_mask[:, :, None].astype(jnp.float32), axis=1)
    shrunk_tok = lax.psum(shrunk_mine, "adapter").astype(jnp.bfloat16)
    adapter_hot = (
        request_adapter_index[:, None] == jnp.arange(adapter_bank, dtype=jnp.int32)[None, :]
    ).astype(jnp.bfloat16)
    spread = (adapter_hot[:, :, None] * shrunk_tok[:, None, :]).reshape(
        segment_rows, adapter_bank * adapter_rank_width
    )
    adapter_update = jnp.dot(
        spread,
        adapter_up_weight[0].reshape(adapter_bank * adapter_rank_width, column_list),
        preferred_element_type=jnp.float32,
    )
    query_rows = (base_query + adapter_scale * adapter_update).astype(jnp.bfloat16)
    own_queries = lax.all_to_all(query_rows, "adapter", split_axis=0, concat_axis=1, tiled=True)
    own_lengths = lax.dynamic_slice_in_dim(cache_valid_length, position * tok_dev, tok_dev)
    group_size = HEADS // KVH
    query_heads = own_queries.reshape(tok_dev, KVH, group_size, HD)
    cached_keys = key_value_cache[:, 0].reshape(tok_dev, CTX, KVH, HD)
    cached_values = key_value_cache[:, 1].reshape(tok_dev, CTX, KVH, HD)
    scores = jnp.einsum(
        "tkgd,tckd->tkgc", query_heads, cached_keys, preferred_element_type=jnp.float32
    ) * HD ** (-0.5)
    is_live = jnp.arange(CTX, dtype=jnp.int32)[None, :] < own_lengths[:, None]
    scores = jnp.where(is_live[:, None, None, :], scores, -jnp.inf)
    row_max = jnp.max(scores, axis=-1, keepdims=True)
    expsum = jnp.exp(scores - row_max)
    probs = (expsum / jnp.sum(expsum, axis=-1, keepdims=True)).astype(jnp.bfloat16)
    context = jnp.einsum(
        "tkgc,tckd->tkgd", probs, cached_values, preferred_element_type=jnp.float32
    )
    return context.astype(jnp.bfloat16).reshape(tok_dev, MODEL_WIDTH)


def solution(mesh):
    in_specs = (
        P(("segment", "adapter"), None),
        P("segment", None),
        P("segment", None, "adapter"),
        P("segment", "adapter", None, None),
        P("segment", None, None, "adapter"),
        P("segment"),
        P("segment"),
        P(("segment", "adapter"), None, None, None),
    )
    out_specs = P(("segment", "adapter"), None)
    return jax.shard_map(body, mesh=mesh, in_specs=in_specs, out_specs=out_specs, check_vma=False)
```

profile of v0, /device:TPU:2, one launch (start us, length us, event | category | flops | bytes accessed | tf_op | source)
XLA Modules:
  0.0 437.0 jit_solution(6237502555371092495)
XLA Ops:
  6.5 0.0 copy-start
  6.5 0.0 collective-permute-start
  6.5 4.6 %collective-permute-done = bf16[8,8192]{1,0:T(8,128)(2,1)S(1)} collective-permute-done((bf16[8,8192]{1,0:T(8,128)(2,1)}, bf16[8,8192]{1,0:T(8,128)(2,1)S(1)}, u32[]{:S(2)}, u32[]{:S(2)}) %collective-permute-start) | collective-permute-done | bytes 131104 | tf_op jit(solution)/shard_map/ppermute | solution.py:19
  11.1 0.2 fusion.11
  11.3 1.5 fusion.13
  12.8 0.0 all-gather.2.cloned.1.call-update
  12.9 0.7 compare_convert_fusion
  13.6 0.7 fusion.19
  14.3 102.8 %all-gather.2.cloned.1.call-done = bf16[512,8192]{1,0:T(8,128)(2,1)} async-done(((bf16[8,8192]{1,0:T(8,128)(2,1)}), bf16[512,8192]{1,0:T(8,128)(2,1)}) %all-gather.2.cloned.1.call-update) | async-done | bytes 8388624 | tf_op jit(solution)/shard_map/all_gather | solution.py:49
  117.0 6.3 %convolution_multiply_fusion.2 = f32[512,64]{0,1:T(8,128)S(1)} fusion(bf16[512,8192]{1,0:T(8,128)(2,1)} %all-gather.2.cloned.1.call-done, bf16[1,1,8192,64]{2,3,1,0:T(8,128)(2,1)} %param.11, f32[512]{0:T(512)S(1)} %compare_convert_fusion), kind=kOutput, calls=%fused_computation.14 | convolution fusion | flops 536903680 | bytes 9570304 | tf_op jit(solution)/shard_map/td,adr->tar/dot_general | solution.py:51
  123.3 277.7 %all-reduce.1 = bf16[512,64]{0,1:T(8,128)(2,1)S(1)} all-reduce(f32[512,64]{0,1:T(8,128)S(1)} %convolution_multiply_fusion.2), channel_id=1, replica_groups=mesh['segment'=8,'adapter'=64] {'adapter'}, use_global_device_ids=true, to_apply=%region_1.2 | all-reduce | flops 32768 | bytes 196608 | tf_op jit(solution)/shard_map/psum | solution.py:61
  401.0 0.3 broadcast_multiply_fusion
  401.3 0.0 copy-start.1
  401.3 5.8 %fusion.1 = f32[512,128]{1,0:T(8,128)S(1)} fusion(bf16[512,8192]{1,0:T(8,128)(2,1)} %all-gather.2.cloned.1.call-done, bf16[1,8192,128]{2,1,0:T(8,128)(2,1)S(1)} %copy-done), kind=kOutput, calls=%fused_computation.1 | convolution fusion | flops 1073741824 | bytes 10747904 | tf_op jit(solution)/shard_map/dot_general | solution.py:50
  407.1 0.0 copy-start.2
  407.1 2.0 fusion.9
  409.1 6.2 %all-to-all-start = ((bf16[64,8,128]{2,1,0:T(8,128)(2,1)}), bf16[64,8,128]{2,1,0:T(8,128)(2,1)S(1)}, u32[]{:S(2)}, u32[]{:S(2)}) async-start(bf16[64,8,128]{2,1,0:T(8,128)(2,1)} %fusion.9), calls=%async_computation | async-start | bytes 262144 | tf_op jit(solution)/shard_map/all_to_all | solution.py:74
  415.5 0.8 dynamic_slice.3
  416.2 0.1 iota_compare_fusion.1
  416.3 11.7 %all-to-all-done = bf16[64,8,128]{2,1,0:T(8,128)(2,1)S(1)} async-done(((bf16[64,8,128]{2,1,0:T(8,128)(2,1)}), bf16[64,8,128]{2,1,0:T(8,128)(2,1)S(1)}, u32[]{:S(2)}, u32[]{:S(2)}) %all-to-all-start) | async-done | bytes 131104 | tf_op jit(solution)/shard_map/all_to_all | solution.py:74
  428.0 0.3 fusion.4
  428.2 0.2 fusion.21
  428.5 1.0 fusion.8
  429.5 0.7 copy.26
  (8 shorter events, 0.1 us)
Async XLA Ops:
  6.5 394.7 %copy-start = (bf16[1,8192,128]{2,1,0:T(8,128)(2,1)S(1)}, bf16[1,8192,128]{2,1,0:T(8,128)(2,1)}, u32[]{:S(2)}) copy-start(bf16[1,8192,128]{2,1,0:T(8,128)(2,1)} %param.10) | copy-start | bytes 6291460
  6.5 110.5 %all-gather.2.cloned.1.call-start = ((), (), s32[]{:S(2)}) async-start(), calls=%async_computation.1 | async-start | bytes 8519680 | tf_op jit(solution)/shard_map/all_gather | solution.py:49
  6.5 4.6 %collective-permute-start = (bf16[8,8192]{1,0:T(8,128)(2,1)}, bf16[8,8192]{1,0:T(8,128)(2,1)S(1)}, u32[]{:S(2)}, u32[]{:S(2)}) collective-permute-start(bf16[8,8192]{1,0:T(8,128)(2,1)} %param.8), channel_id=1, source_target_pairs={{0,64},{64,128},{128,192},{192,256},{256,320},{320,384},{384,448},... | collective-permute-start | bytes 393224 | tf_op jit(solution)/shard_map/ppermute | solution.py:19
  401.3 5.8 %copy-start.1 = (bf16[1,64,64,128]{3,2,1,0:T(8,128)(2,1)S(1)}, bf16[1,64,64,128]{3,2,1,0:T(8,128)(2,1)}, u32[]{:S(2)}) copy-start(bf16[1,64,64,128]{3,2,1,0:T(8,128)(2,1)} %param.12) | copy-start | bytes 3145732
  407.1 8.2 %copy-start.2 = (bf16[8,2,16,1024]{3,2,1,0:T(8,128)(2,1)S(1)}, bf16[8,2,16,1024]{3,2,1,0:T(8,128)(2,1)}, u32[]{:S(2)}) copy-start(bf16[8,2,16,1024]{3,2,1,0:T(8,128)(2,1)} %param.15) | copy-start | bytes 1572868
  409.1 18.9 %all-to-all-start = ((bf16[64,8,128]{2,1,0:T(8,128)(2,1)}), bf16[64,8,128]{2,1,0:T(8,128)(2,1)S(1)}, u32[]{:S(2)}, u32[]{:S(2)}) async-start(bf16[64,8,128]{2,1,0:T(8,128)(2,1)} %fusion.9), calls=%async_computation | async-start | bytes 262144 | tf_op jit(solution)/shard_map/all_to_all | solution.py:74
Sparse Core Ops, SparseCore 0:
  13.0 103.9 all-gather.1
where the time goes:
time: 437 us
  blocking collectives  278 us (64%)
  waiting for transfers between devices  119 us (27%)
  matrix products  15.3 us (4%)
  between operations  13.5 us (3%)
  starting transfers between devices  6.2 us (1%)
    psum x1, blocking collectives, body(): shrunk_tok = lax.psum(shrunk_mine, 'adapter').astype(jnp.bfloat16)  278 us
    all_gather x1, waiting for transfers between devices, body(): row_piece = lax.all_gather(normalized_input, 'adapter', axis=0, tiled=True)  103 us
    all_to_all x1, waiting for transfers between devices, body(): lax.all_to_all(query_rows, 'adapter', split_axis=0, concat_axis=1, tiled=...  11.7 us
  transfers between devices with their start and end apart: 3, of which 3 were waited for; matrix products, arithmetic and copies ran while one was open for 1% of the time, Pallas kernels for 0%

commit v1 on v0

--- a/solution.py
+++ b/solution.py
@@ -8,15 +8,37 @@
 KVH = 8
 HD = 128
 CTX = 16
+SIDE = 8
+OWN_MAX = 32
 
 
 adapter_scale = 0.5
 norm_eps = 1e-05
 
+BOTH = ("segment", "adapter")
+
+
+def line_groups(segments, second):
+    groups = []
+    for s in range(segments):
+        along_minor = (s % 2 == 0) != second
+        for i in range(SIDE):
+            if along_minor:
+                groups.append([s * 64 + i * SIDE + j for j in range(SIDE)])
+            else:
+                groups.append([s * 64 + j * SIDE + i for j in range(SIDE)])
+    return groups
+
 
 def from_behind(value, axis, by):
     devices = lax.axis_size(axis)
     return lax.ppermute(value, axis, [(i, (i + by) % devices) for i in range(devices)])
+
+
+def swap_sides(odd, value):
+    shape = value.shape
+    cut = value.reshape((SIDE, SIDE, -1) + shape[1:])
+    return jnp.where(odd, cut.swapaxes(0, 1), cut).reshape(shape)
 
 
 def body(
@@ -29,6 +51,9 @@
     cache_valid_length,
     key_value_cache,
 ):
+    segments = lax.axis_size("segment")
+    position = lax.axis_index("adapter")
+    odd = lax.axis_index("segment") % 2 == 1
     received_rows = from_behind(incoming, "segment", 1)
     values = received_rows.astype(jnp.float32)
     mean_square = jnp.mean(values * values, axis=-1, keepdims=True)
@@ -36,41 +61,62 @@
         jnp.bfloat16
     )
     tok_dev = received_rows.shape[0]
-    position = lax.axis_index("adapter")
     segment_rows = request_adapter_index.shape[0]
     weight = query_weight[0]
     column_list = weight.shape[1]
-    down_matrices = adapter_down_weight[0]
-    ad_dev = down_matrices.shape[0]
-    adapter_rank_width = down_matrices.shape[2]
-    adapter_bank = adapter_up_weight.shape[1]
-    owner_of = request_adapter_index // ad_dev
-    local_of = request_adapter_index % ad_dev
-    row_piece = lax.all_gather(normalized_input, "adapter", axis=0, tiled=True)
-    plain = jnp.dot(row_piece, weight, preferred_element_type=jnp.float32)
-    shrunk = jnp.einsum("td,adr->tar", row_piece, down_matrices, preferred_element_type=jnp.float32)
-    projected = jnp.concatenate(
-        [plain, shrunk.reshape(row_piece.shape[0], ad_dev * adapter_rank_width)], axis=1
+    down = adapter_down_weight[0, 0]
+    rank_width = down.shape[1]
+    bank = adapter_up_weight.shape[1]
+
+    line = lax.all_to_all(
+        jnp.broadcast_to(normalized_input[None], (SIDE, tok_dev, MODEL_WIDTH)),
+        BOTH,
+        split_axis=0,
+        concat_axis=0,
+        tiled=True,
+        axis_index_groups=line_groups(segments, False),
+    ).reshape(SIDE * tok_dev, MODEL_WIDTH)
+    rows = lax.all_gather(
+        line, BOTH, axis=0, tiled=True, axis_index_groups=line_groups(segments, True)
     )
-    base_query = projected[:, :column_list]
-    shrunk_all = projected[:, column_list:].reshape(segment_rows, ad_dev, adapter_rank_width)
-    select_mask = (local_of[:, None] == jnp.arange(ad_dev, dtype=jnp.int32)[None, :]) & (
-        owner_of == position
-    )[:, None]
-    shrunk_mine = jnp.sum(shrunk_all * select_mask[:, :, None].astype(jnp.float32), axis=1)
-    shrunk_tok = lax.psum(shrunk_mine, "adapter").astype(jnp.bfloat16)
-    adapter_hot = (
-        request_adapter_index[:, None] == jnp.arange(adapter_bank, dtype=jnp.int32)[None, :]
+
+    index = swap_sides(odd, request_adapter_index)
+    hot = index[:, None] == jnp.arange(bank, dtype=jnp.int32)[None, :]
+    hot_counts = jnp.cumsum(hot.astype(jnp.int32), axis=0)
+    slot = jnp.sum(jnp.where(hot, hot_counts, 0), axis=1) - 1
+    pick = (
+        (jnp.arange(OWN_MAX, dtype=jnp.int32)[:, None] == slot[None, :])
+        & (index == position)[None, :]
     ).astype(jnp.bfloat16)
-    spread = (adapter_hot[:, :, None] * shrunk_tok[:, None, :]).reshape(
-        segment_rows, adapter_bank * adapter_rank_width
+    place = (
+        (index * OWN_MAX + slot)[:, None]
+        == jnp.arange(bank * OWN_MAX, dtype=jnp.int32)[None, :]
+    ).astype(jnp.bfloat16)
+
+    shrunk_all = jnp.dot(rows, down, preferred_element_type=jnp.float32).astype(jnp.bfloat16)
+    shrunk_mine = jnp.dot(pick, shrunk_all, preferred_element_type=jnp.float32).astype(jnp.bfloat16)
+    flat = shrunk_mine.reshape(1, OWN_MAX * rank_width)
+    shrunk_slots = lax.all_to_all(
+        jnp.broadcast_to(flat, (bank, OWN_MAX * rank_width)),
+        "adapter",
+        split_axis=0,
+        concat_axis=0,
+        tiled=True,
+    ).reshape(bank * OWN_MAX, rank_width)
+    base_query = jnp.dot(rows, weight, preferred_element_type=jnp.float32)
+    shrunk_tok = jnp.dot(place, shrunk_slots, preferred_element_type=jnp.float32).astype(
+        jnp.bfloat16
+    )
+    spread = (hot.astype(jnp.bfloat16)[:, :, None] * shrunk_tok[:, None, :]).reshape(
+        segment_rows, bank * rank_width
     )
     adapter_update = jnp.dot(
         spread,
-        adapter_up_weight[0].reshape(adapter_bank * adapter_rank_width, column_list),
+        adapter_up_weight[0].reshape(bank * rank_width, column_list),
         preferred_element_type=jnp.float32,
     )
     query_rows = (base_query + adapter_scale * adapter_update).astype(jnp.bfloat16)
+    query_rows = swap_sides(odd, query_rows)
     own_queries = lax.all_to_all(query_rows, "adapter", split_axis=0, concat_axis=1, tiled=True)
     own_lengths = lax.dynamic_slice_in_dim(cache_valid_length, position * tok_dev, tok_dev)
     group_size = HEADS // KVH

time: 437 us -> 164 us (0.38)
  blocking collectives: 278 us -> 25.9 us
  waiting for transfers between devices: 119 us -> 81.3 us
  starting transfers between devices: 6.2 us -> 14.9 us
    psum x1 -> x0, blocking collectives: 278 us -> none  [body(): shrunk_tok = lax.psum(shrunk_mine, 'adapter').astype(jnp.bfloat16)]
    all_gather x1, waiting for transfers between devices: 103 us -> 56.2 us  [body(): lax.all_gather(line, BOTH, axis=0, tiled=True, axis_index_groups=line_gro...]
    all_to_all x0 -> x1, blocking collectives: none -> 25.9 us  [body(): lax.all_to_all(jnp.broadcast_to(normalized_input[None], (SIDE, tok_dev, M...]
    all_to_all x0 -> x1, starting transfers between devices: none -> 10.2 us  [body(): lax.all_to_all(jnp.broadcast_to(flat, (bank, OWN_MAX * rank_width)), 'ada...]
    all_to_all x0 -> x1, waiting for transfers between devices: none -> 8.75 us  [body(): lax.all_to_all(jnp.broadcast_to(flat, (bank, OWN_MAX * rank_width)), 'ada...]
    dot_general x3 -> x4, matrix products: 14 us -> 14.2 us  [the longest x1 6.17 us: body(): jnp.dot(pick, shrunk_all, preferred_element_type=jnp.float32)]
  transfers between devices with their start and end apart: 3 -> 4, of which waited for: 3 -> 4; matrix products, arithmetic and copies ran while one was open for 1% -> 5% of each run, Pallas kernels for 0% -> 0%
where the time goes in v1:
time: 164 us; the launch traced here: 163 us
  waiting for transfers between devices  81.3 us (50%)
  blocking collectives  25.9 us (16%)
  matrix products  15.4 us (9%)
  starting transfers between devices  14.9 us (9%)
  between operations  13.7 us (8%)
  other arithmetic  7.39 us (5%)
  local copies, waits for them, and re-layouts  4.73 us (3%)
    all_gather x1, waiting for transfers between devices, body(): lax.all_gather(line, BOTH, axis=0, tiled=True, axis_index_groups=line_gro...  56.2 us
    all_to_all x1, blocking collectives, body(): lax.all_to_all(jnp.broadcast_to(normalized_input[None], (SIDE, tok_dev, M...  25.9 us
    all_to_all x1, waiting for transfers between devices, body(): lax.all_to_all(query_rows, 'adapter', split_axis=0, concat_axis=1, tiled=...  11.7 us
    all_to_all x1, starting transfers between devices, body(): lax.all_to_all(jnp.broadcast_to(flat, (bank, OWN_MAX * rank_width)), 'ada...  10.2 us
    all_to_all x1, waiting for transfers between devices, body(): lax.all_to_all(jnp.broadcast_to(flat, (bank, OWN_MAX * rank_width)), 'ada...  8.75 us
    dot_general x1, matrix products, body(): jnp.dot(pick, shrunk_all, preferred_element_type=jnp.float32)  6.17 us
    dot_general x1, matrix products, body(): base_query = jnp.dot(rows, weight, preferred_element_type=jnp.float32)  5.7 us
    all_to_all x1, starting transfers between devices, body(): lax.all_to_all(query_rows, 'adapter', split_axis=0, concat_axis=1, tiled=...  4.62 us
  transfers between devices with their start and end apart: 4, of which 4 were waited for; matrix products, arithmetic and copies ran while one was open for 5% of the time, Pallas kernels for 0%

profile of v1, /device:TPU:2, one launch (start us, length us, event | category | flops | bytes accessed | tf_op | source)
XLA Modules:
  0.0 163.3 jit_solution(515998053342328657)
XLA Ops:
  6.6 4.6 %collective-permute-done = bf16[8,8192]{1,0:T(8,128)(2,1)S(1)} collective-permute-done((bf16[8,8192]{1,0:T(8,128)(2,1)}, bf16[8,8192]{1,0:T(8,128)(2,1)S(1)}, u32[]{:S(2)}, u32[]{:S(2)}) %collective-permute-start) | collective-permute-done | bytes 131104 | tf_op jit(solution)/shard_map/ppermute | solution.py:35
  11.4 0.9 fusion.18
  12.3 25.9 %all_to_all.27 = bf16[8,8,8192]{2,1,0:T(8,128)(2,1)} all-to-all(bf16[8,8,8192]{2,1,0:T(8,128)(2,1)S(1)} %broadcast_in_dim.19), channel_id=1, replica_groups={{0,1,2,3,4,5,6,7},{8,9,10,11,12,13,14,15},{16,17,18,19,20,21,22,23},{24..., dimensions={0} | all-to-all | bytes 2097152 | tf_op jit(solution)/shard_map/all_to_all | solution.py:71
  38.6 1.2 reduce-window.6
  40.2 56.2 %all-gather.2.cloned.1.call-done = bf16[512,8192]{1,0:T(8,128)(2,1)} async-done(((bf16[64,8192]{1,0:T(8,128)(2,1)}), bf16[512,8192]{1,0:T(8,128)(2,1)}) %all-gather.2.cloned.1.call-update) | async-done | bytes 8388624 | tf_op jit(solution)/shard_map/all_gather | solution.py:79
  96.4 6.2 %fusion.13 = bf16[32,64]{1,0:T(8,128)(2,1)S(1)} fusion(bf16[512,8192]{1,0:T(8,128)(2,1)} %all-gather.2.cloned.1.call-done, bf16[1,1,8192,64]{2,3,1,0:T(8,128)(2,1)S(1)} %copy-done.1, s32[512]{0:T(512)S(1)} %get-tuple-element.8, pred[512]{0:T(512)(128)(4,1)S(1)} %broadcast_compare_fusion), kind=kOutput, calls=%fused_computation.19 | convolution fusion | flops 539035648 | bytes 9443840 | tf_op jit(solution)/shard_map/dot_general | solution.py:97
  102.7 0.3 broadcast_in_dim.22
  103.0 0.5 broadcast.98
  103.5 2.2 %reduce.3 = bf16[64,2048]{1,0:T(8,128)(2,1)S(1)} reduce(bf16[64,1,2048]{2,1,0:T(2,128)(2,1)S(1)} %broadcast_in_dim.22, bf16[]{:T(256)} %broadcast.98), dimensions={1}, to_apply=%broadcast_in_dim.22.reduce_sub_computation | reduce | bytes 524290 | tf_op jit(solution)/shard_map/broadcast_in_dim | solution.py:100
  105.6 0.9 reshape.144
  106.5 10.2 %all-to-all-start.1 = ((bf16[64,2,1024]{2,1,0:T(2,128)(2,1)}), bf16[64,2,1024]{2,1,0:T(2,128)(2,1)S(1)}, u32[]{:S(2)}, u32[]{:S(2)}) async-start(bf16[64,2,1024]{2,1,0:T(2,128)(2,1)} %reshape.144), calls=%async_computation.1 | async-start | bytes 524288 | tf_op jit(solution)/shard_map/all_to_all | solution.py:99
  116.8 5.7 %fusion.2 = f32[512,128]{1,0:T(8,128)S(1)} fusion(bf16[512,8192]{1,0:T(8,128)(2,1)} %all-gather.2.cloned.1.call-done, bf16[1,8192,128]{2,1,0:T(8,128)(2,1)S(1)} %copy-done), kind=kOutput, calls=%fused_computation.3 | convolution fusion | flops 1073741824 | bytes 10747904 | tf_op jit(solution)/shard_map/dot_general | solution.py:106
  122.5 8.8 %all-to-all-done.1 = bf16[64,2,1024]{2,1,0:T(2,128)(2,1)S(1)} async-done(((bf16[64,2,1024]{2,1,0:T(2,128)(2,1)}), bf16[64,2,1024]{2,1,0:T(2,128)(2,1)S(1)}, u32[]{:S(2)}, u32[]{:S(2)}) %all-to-all-start.1) | async-done | bytes 262176 | tf_op jit(solution)/shard_map/all_to_all | solution.py:99
  131.5 1.5 reduce.1
  133.0 0.5 reshape.138
  133.5 1.0 fusion.11
  134.5 0.3 broadcast_multiply_fusion
  134.8 1.3 fusion.9
  136.1 0.7 bitcast_select_fusion
  136.8 4.6 %all-to-all-start.2 = ((bf16[64,8,128]{2,1,0:T(8,128)(2,1)}), bf16[64,8,128]{2,1,0:T(8,128)(2,1)S(1)}, u32[]{:S(2)}, u32[]{:S(2)}) async-start(bf16[64,8,128]{2,1,0:T(8,128)(2,1)} %bitcast.10), calls=%async_computation.2 | async-start | bytes 262144 | tf_op jit(solution)/shard_map/all_to_all | solution.py:120
  141.6 0.8 dynamic_slice.3
  142.4 11.7 %all-to-all-done.2 = bf16[64,8,128]{2,1,0:T(8,128)(2,1)S(1)} async-done(((bf16[64,8,128]{2,1,0:T(8,128)(2,1)}), bf16[64,8,128]{2,1,0:T(8,128)(2,1)S(1)}, u32[]{:S(2)}, u32[]{:S(2)}) %all-to-all-start.2) | async-done | bytes 131104 | tf_op jit(solution)/shard_map/all_to_all | solution.py:120
  154.7 1.0 fusion.10
  155.7 0.7 copy.41
  (36 shorter events, 2.0 us)
Async XLA Ops:
  6.5 110.2 %copy-start = (bf16[1,8192,128]{2,1,0:T(8,128)(2,1)S(1)}, bf16[1,8192,128]{2,1,0:T(8,128)(2,1)}, u32[]{:S(2)}) copy-start(bf16[1,8192,128]{2,1,0:T(8,128)(2,1)} %param.10) | copy-start | bytes 6291460
  6.5 31.7 %copy-start.4 = (s32[512]{0:T(512)S(1)}, s32[512]{0:T(512)}, u32[]{:S(2)}) copy-start(s32[512]{0:T(512)} %param.13) | copy-start | bytes 6148
  6.5 89.9 %copy-start.1 = (bf16[1,1,8192,64]{2,3,1,0:T(8,128)(2,1)S(1)}, bf16[1,1,8192,64]{2,3,1,0:T(8,128)(2,1)}, u32[]{:S(2)}) copy-start(bf16[1,1,8192,64]{2,3,1,0:T(8,128)(2,1)} %param.11) | copy-start | bytes 3145732
  6.5 89.9 %all-gather.2.cloned.1.call-start = ((), (), s32[]{:S(2)}) async-start(), calls=%async_computation.3 | async-start | bytes 9437184 | tf_op jit(solution)/shard_map/all_gather | solution.py:79
  6.5 4.6 %collective-permute-start = (bf16[8,8192]{1,0:T(8,128)(2,1)}, bf16[8,8192]{1,0:T(8,128)(2,1)S(1)}, u32[]{:S(2)}, u32[]{:S(2)}) collective-permute-start(bf16[8,8192]{1,0:T(8,128)(2,1)} %param.8), channel_id=1, source_target_pairs={{0,64},{64,128},{128,192},{192,256},{256,320},{320,384},{384,448},... | collective-permute-start | bytes 393224 | tf_op jit(solution)/shard_map/ppermute | solution.py:35
  106.5 24.7 %all-to-all-start.1 = ((bf16[64,2,1024]{2,1,0:T(2,128)(2,1)}), bf16[64,2,1024]{2,1,0:T(2,128)(2,1)S(1)}, u32[]{:S(2)}, u32[]{:S(2)}) async-start(bf16[64,2,1024]{2,1,0:T(2,128)(2,1)} %reshape.144), calls=%async_computation.1 | async-start | bytes 524288 | tf_op jit(solution)/shard_map/all_to_all | solution.py:99
  133.5 1.3 copy-start.2
  134.5 6.9 %copy-start.3 = (bf16[8,2,16,1024]{3,2,1,0:T(8,128)(2,1)S(1)}, bf16[8,2,16,1024]{3,2,1,0:T(8,128)(2,1)}, u32[]{:S(2)}) copy-start(bf16[8,2,16,1024]{3,2,1,0:T(8,128)(2,1)} %param.15) | copy-start | bytes 1572868
  136.8 17.4 %all-to-all-start.2 = ((bf16[64,8,128]{2,1,0:T(8,128)(2,1)}), bf16[64,8,128]{2,1,0:T(8,128)(2,1)S(1)}, u32[]{:S(2)}, u32[]{:S(2)}) async-start(bf16[64,8,128]{2,1,0:T(8,128)(2,1)} %bitcast.10), calls=%async_computation.2 | async-start | bytes 262144 | tf_op jit(solution)/shard_map/all_to_all | solution.py:120
Sparse Core Ops, SparseCore 0:
  38.4 58.0 all-gather.1

commit v2 on v1

v2 whole, which is shorter than its diff:
```python
import jax
import jax.numpy as jnp
from jax import lax
from jax.experimental import pallas as pl
from jax.experimental.pallas import tpu as pltpu
from jax.sharding import PartitionSpec as P

MODEL_WIDTH = 8192
HEADS = 64
KVH = 8
HD = 128
CTX = 16
SIDE = 8
OWN_MAX = 32


adapter_scale = 0.5
norm_eps = 1e-05

BOTH = ("segment", "adapter")


def line_groups(segments, second):
    groups = []
    for s in range(segments):
        along_minor = (s % 2 == 0) != second
        for i in range(SIDE):
            if along_minor:
                groups.append([s * 64 + i * SIDE + j for j in range(SIDE)])
            else:
                groups.append([s * 64 + j * SIDE + i for j in range(SIDE)])
    return groups


def from_behind(value, axis, by):
    devices = lax.axis_size(axis)
    return lax.ppermute(value, axis, [(i, (i + by) % devices) for i in range(devices)])


def swap_sides(odd, value):
    shape = value.shape
    cut = value.reshape((SIDE, SIDE, -1) + shape[1:])
    return jnp.where(odd, cut.swapaxes(0, 1), cut).reshape(shape)


def over_line(blocks, groups):
    return lax.all_to_all(
        blocks, BOTH, split_axis=0, concat_axis=0, tiled=True, axis_index_groups=groups
    )


def along_line(block, groups, by):
    pairs = [(g[i], g[(i + by) % SIDE]) for g in groups for i in range(SIDE)]
    return lax.ppermute(block, BOTH, pairs)


def to_partner(block, groups):
    pairs = [(g[i], g[i ^ 1]) for g in groups for i in range(SIDE)]
    return lax.ppermute(block, BOTH, pairs)


def shrink_kernel(which_ref, mine_ref, theirs_ref, down_ref, out_ref):
    half = mine_ref.shape[1]
    shrunk = None
    for rows_ref, part in ((mine_ref, which_ref[0]), (theirs_ref, 1 - which_ref[0])):
        start = pl.multiple_of(part * half, half)
        term = lax.dot_general(
            rows_ref[...],
            down_ref[:, pl.ds(start, half)],
            (((1,), (1,)), ((), ())),
            preferred_element_type=jnp.float32,
        )
        shrunk = term if shrunk is None else shrunk + term
    some = OWN_MAX // 2
    shrunk = shrunk.astype(jnp.bfloat16)
    flat = jnp.concatenate([shrunk[:some], shrunk[some:]], axis=1)
    out_ref[...] = jnp.broadcast_to(flat[None], out_ref.shape)


def shrink(which, mine, theirs, down_t, bank):
    vmem = pl.BlockSpec(memory_space=pltpu.VMEM)
    return pl.pallas_call(
        shrink_kernel,
        out_shape=jax.ShapeDtypeStruct((bank, OWN_MAX // 2, 2 * down_t.shape[0]), jnp.bfloat16),
        in_specs=[pl.BlockSpec(memory_space=pltpu.SMEM), vmem, vmem, vmem],
        out_specs=vmem,
        compiler_params=pltpu.CompilerParams(vmem_limit_bytes=8 * 1024 * 1024),
    )(which.reshape(1), mine, theirs, down_t)


def body(
    incoming,
    attention_norm_gain,
    query_weight,
    adapter_down_weight,
    adapter_up_weight,
    request_adapter_index,
    cache_valid_length,
    key_value_cache,
):
    segments = lax.axis_size("segment")
    position = lax.axis_index("adapter")
    odd = lax.axis_index("segment") % 2 == 1
    lines_b = line_groups(segments, False)
    lines_a = line_groups(segments, True)
    minor, major = position % SIDE, position // SIDE
    at_a = jnp.where(odd, minor, major)
    at_b = jnp.where(odd, major, minor)
    which = at_b % 2
    weight = query_weight[0]
    column_list = weight.shape[1]
    down = adapter_down_weight[0, 0]
    rank_width = down.shape[1]
    bank = adapter_up_weight.shape[1]
    segment_rows = request_adapter_index.shape[0]
    half = MODEL_WIDTH // 2

    received_rows = from_behind(incoming, "segment", 1)

    weight_theirs = to_partner(
        lax.dynamic_slice_in_dim(weight, (1 - which) * half, half), lines_b
    )

    tok_dev = received_rows.shape[0]
    line_rows = SIDE * tok_dev
    values = received_rows.astype(jnp.float32)
    mean_square = jnp.mean(values * values, axis=-1, keepdims=True)
    normalized_input = (values * lax.rsqrt(mean_square + norm_eps) * attention_norm_gain[0]).astype(
        jnp.bfloat16
    )
    cut = normalized_input.reshape(tok_dev, 2, half).swapaxes(0, 1)
    line = over_line(
        jnp.broadcast_to(cut[None], (SIDE // 2, 2, tok_dev, half)).reshape(SIDE, tok_dev, half),
        lines_b,
    ).reshape(line_rows, half)

    normalized_input, weight, request_adapter_index = lax.optimization_barrier(
        (normalized_input, weight, request_adapter_index)
    )
    weight_both = lax.optimization_barrier(
        jnp.concatenate(
            [lax.dynamic_slice_in_dim(weight, which * half, half), weight_theirs], axis=1
        )
    )

    quarter = half // 2
    blocks = [None] * SIDE
    blocks[0] = ahead = behind = line
    for step in range(1, SIDE // 2):
        ahead = along_line(ahead, lines_a, 1)
        behind = along_line(behind, lines_a, -1)
        blocks[SIDE - step], blocks[step] = ahead, behind
    far_low = along_line(ahead[:, :quarter], lines_a, 1)
    far_high = along_line(behind[:, quarter:], lines_a, -1)

    adapters = jnp.arange(bank, dtype=jnp.int32)[None, :]
    named = request_adapter_index[:, None] == adapters
    counts = jnp.cumsum(named.astype(jnp.int32), axis=0)
    slot = jnp.sum(jnp.where(named, counts, 0), axis=1) - 1
    both = jnp.stack([request_adapter_index, slot], axis=1)
    both = swap_sides(odd, both).reshape(SIDE, line_rows, 2)
    both = jnp.roll(both, -at_a, axis=0).reshape(segment_rows, 2)
    index, slot = both[:, 0], both[:, 1]
    hot = index[:, None] == adapters
    partner = jnp.where(odd, position + SIDE * (1 - 2 * which), position + (1 - 2 * which))
    owners = jnp.stack([position, partner])
    pick = (
        (jnp.arange(OWN_MAX, dtype=jnp.int32)[None, :, None] == slot[None, None, :])
        & (index[None, None, :] == owners[:, None, None])
    ).astype(jnp.bfloat16).reshape(2 * OWN_MAX, SIDE, line_rows)
    some = OWN_MAX // 2
    place = (
        (index * some + slot % some)[:, None]
        == jnp.arange(bank * some, dtype=jnp.int32)[None, :]
    ).astype(jnp.bfloat16)

    def pick_from(j, block):
        return jnp.dot(pick[:, j], block, preferred_element_type=jnp.float32).astype(jnp.bfloat16)

    picked = pick_from(0, line)
    for step in range(1, SIDE // 2):
        for j in (SIDE - step, step):
            picked = picked + pick_from(j, blocks[j])
    far = SIDE // 2
    picked = picked + jnp.concatenate(
        [pick_from(far, far_low), pick_from(far, far_high)], axis=1
    )
    picked_theirs = to_partner(picked[OWN_MAX:], lines_b)
    shrunk = shrink(which, picked[:OWN_MAX], picked_theirs, down.T, bank)
    def times(block, low=0, high=half):
        return jnp.dot(block, weight_both[low:high], preferred_element_type=jnp.float32)

    products = [None if block is None else times(block) for block in blocks]
    products[far] = times(far_low, 0, quarter) + times(far_high, quarter, half)
    product = jnp.concatenate(products, axis=0)
    shrunk, product = lax.optimization_barrier((shrunk, product))
    slots = lax.all_to_all(
        shrunk,
        "adapter",
        split_axis=0,
        concat_axis=0,
        tiled=True,
    ).reshape(bank * some, 2 * rank_width)

    base_query = product[:, :column_list] + to_partner(product[:, column_list:], lines_b)
    both = jnp.dot(place, slots, preferred_element_type=jnp.float32).astype(jnp.bfloat16)
    shrunk_tok = jnp.where((slot < some)[:, None], both[:, :rank_width], both[:, rank_width:])
    spread = (hot.astype(jnp.bfloat16)[:, :, None] * shrunk_tok[:, None, :]).reshape(
        segment_rows, bank * rank_width
    )
    adapter_update = jnp.dot(
        spread,
        adapter_up_weight[0].reshape(bank * rank_width, column_list),
        preferred_element_type=jnp.float32,
    )
    query_rows = (base_query + adapter_scale * adapter_update).astype(jnp.bfloat16)
    query_rows = query_rows.reshape(SIDE, line_rows, column_list)
    query_rows = jnp.roll(query_rows, at_a, axis=0)
    query_rows = swap_sides(odd, query_rows.reshape(segment_rows, column_list))
    own_queries = lax.all_to_all(
        query_rows.reshape(HEADS, tok_dev, HD), "adapter", split_axis=0, concat_axis=0, tiled=True
    )
    own_lengths = lax.dynamic_slice_in_dim(cache_valid_length, position * tok_dev, tok_dev)
    group_size = HEADS // KVH
    query_heads = own_queries.reshape(KVH, group_size, tok_dev, HD)
    cached_keys = key_value_cache[:, 0].reshape(tok_dev, CTX, KVH, HD)
    cached_values = key_value_cache[:, 1].reshape(tok_dev, CTX, KVH, HD)
    scores = jnp.einsum(
        "kgtd,tckd->tkgc", query_heads, cached_keys, preferred_element_type=jnp.float32
    ) * HD ** (-0.5)
    is_live = jnp.arange(CTX, dtype=jnp.int32)[None, :] < own_lengths[:, None]
    scores = jnp.where(is_live[:, None, None, :], scores, -jnp.inf)
    row_max = jnp.max(scores, axis=-1, keepdims=True)
    expsum = jnp.exp(scores - row_max)
    probs = (expsum / jnp.sum(expsum, axis=-1, keepdims=True)).astype(jnp.bfloat16)
    context = jnp.einsum(
        "tkgc,tckd->tkgd", probs, cached_values, preferred_element_type=jnp.float32
    )
    return context.astype(jnp.bfloat16).reshape(tok_dev, MODEL_WIDTH)


def solution(mesh):
    in_specs = (
        P(("segment", "adapter"), None),
        P("segment", None),
        P("segment", None, "adapter"),
        P("segment", "adapter", None, None),
        P("segment", None, None, "adapter"),
        P("segment"),
        P("segment"),
        P(("segment", "adapter"), None, None, None),
    )
    out_specs = P(("segment", "adapter"), None)
    return jax.shard_map(body, mesh=mesh, in_specs=in_specs, out_specs=out_specs, check_vma=False)
```

time: 164 us -> 141 us (0.86)
  starting transfers between devices: 14.9 us -> 62.3 us
  waiting for transfers between devices: 81.3 us -> 53.1 us
  blocking collectives: 25.9 us -> 0 us
  between operations: 13.7 us -> 0.63 us
  matrix products: 15.4 us -> 9.58 us
  local copies, waits for them, and re-layouts: 4.73 us -> 8.11 us
  other arithmetic: 7.39 us -> 5.06 us
    all_gather x1 -> x0, waiting for transfers between devices: 56.2 us -> none  [body(): lax.all_gather(line, BOTH, axis=0, tiled=True, axis_index_groups=line_gro...]
    ppermute x0 -> x11, starting transfers between devices: none -> 45 us  [the longest x8 35.4 us: along_line(): return lax.ppermute(block, BOTH, pairs)]
    all_to_all x1 -> x0, blocking collectives: 25.9 us -> none  [body(): lax.all_to_all(jnp.broadcast_to(normalized_input[None], (SIDE, tok_dev, M...]
    ppermute x0 -> x11, waiting for transfers between devices: none -> 19.7 us  [the longest x8 16.1 us: along_line(): return lax.ppermute(block, BOTH, pairs)]
    all_to_all x2 -> x3, waiting for transfers between devices: 20.5 us -> 33.4 us  [the longest x1 11.7 us: body(): lax.all_to_all(query_rows.reshape(HEADS, tok_dev, HD), 'adapter', split_a...]
    dot_general x4 -> x20, matrix products: 13.1 us -> 7.3 us  [the longest x9 3.91 us: times(): jnp.dot(block, weight_both[low:high], preferred_element_type=jnp.float32)]
    ppermute x1, waiting for transfers between devices: 4.59 us -> 0.01 us  [from_behind(): lax.ppermute(value, axis, [(i, (i + by) % devices) for i in range(devices)])]
    all_to_all x2 -> x3, starting transfers between devices: 14.8 us -> 17.3 us  [the longest x1 6.2 us: over_line(): lax.all_to_all(blocks, BOTH, split_axis=0, concat_axis=0, tiled=True, axi...]
  transfers between devices with their start and end apart: 4 -> 15, of which waited for: 4 -> 9; matrix products, arithmetic and copies ran while one was open for 5% -> 11% of each run, Pallas kernels for 0% -> 0%
where the time goes in v2:
time: 141 us; the launch traced here: 140 us
  starting transfers between devices  62.3 us (44%)
  waiting for transfers between devices  53.1 us (38%)
  matrix products  9.58 us (7%)
  local copies, waits for them, and re-layouts  8.11 us (6%)
  other arithmetic  5.06 us (4%)
    ppermute x8, starting transfers between devices, along_line(): return lax.ppermute(block, BOTH, pairs)  35.4 us
    ppermute x8, waiting for transfers between devices, along_line(): return lax.ppermute(block, BOTH, pairs)  16.1 us
    all_to_all x1, waiting for transfers between devices, body(): lax.all_to_all(query_rows.reshape(HEADS, tok_dev, HD), 'adapter', split_a...  11.7 us
    all_to_all x1, waiting for transfers between devices, over_line(): lax.all_to_all(blocks, BOTH, split_axis=0, concat_axis=0, tiled=True, axi...  11.7 us
    all_to_all x1, waiting for transfers between devices, body(): lax.all_to_all(shrunk, 'adapter', split_axis=0, concat_axis=0, tiled=True)  10 us
    ppermute x3, starting transfers between devices, to_partner(): return lax.ppermute(block, BOTH, pairs)  9.58 us
    all_to_all x1, starting transfers between devices, over_line(): lax.all_to_all(blocks, BOTH, split_axis=0, concat_axis=0, tiled=True, axi...  6.2 us
    all_to_all x1, starting transfers between devices, body(): lax.all_to_all(query_rows.reshape(HEADS, tok_dev, HD), 'adapter', split_a...  5.58 us
  transfers between devices with their start and end apart: 15, of which 9 were waited for; matrix products, arithmetic and copies ran while one was open for 11% of the time, Pallas kernels for 0%

profile of v2, /device:TPU:2, one launch (start us, length us, event | category | flops | bytes accessed | tf_op | source)
XLA Modules:
  0.0 139.9 jit_solution(3680009820173465770)
XLA Ops:
  0.1 1.5 %copy-done = bf16[1,8192,128]{2,1,0:T(8,128)(2,1)S(1)} copy-done((bf16[1,8192,128]{2,1,0:T(8,128)(2,1)S(1)}, bf16[1,8192,128]{2,1,0:T(8,128)(2,1)}, u32[]{:S(2)}) %copy-start) | copy-done | bytes 2097176
  2.6 3.5 %collective-permute-start.10 = (bf16[4096,128]{1,0:T(8,128)(2,1)}, bf16[4096,128]{1,0:T(8,128)(2,1)}, u32[]{:S(2)}, u32[]{:S(2)}) collective-permute-start(bf16[4096,128]{1,0:T(8,128)(2,1)} %dynamic-slice_bitcast_fusion), channel_id=1, source_target_pairs={{0,1},{1,0},{2,3},{3,2},{4,5},{5,4},{6,7},{7,6},{8,9},{9,8},{10,11... | collective-permute-start | bytes 3145736 | tf_op jit(solution)/shard_map/ppermute | solution.py:59
  7.4 6.2 %all-to-all-start = ((bf16[8,8,4096]{2,1,0:T(8,128)(2,1)}), bf16[8,8,4096]{2,1,0:T(8,128)(2,1)S(1)}, u32[]{:S(2)}, u32[]{:S(2)}) async-start(bf16[8,8,4096]{2,1,0:T(8,128)(2,1)} %bitcast.12), calls=%async_computation | async-start | bytes 1048576 | tf_op jit(solution)/shard_map/all_to_all | solution.py:47
  17.3 11.7 %all-to-all-done = bf16[8,8,4096]{2,1,0:T(8,128)(2,1)S(1)} async-done(((bf16[8,8,4096]{2,1,0:T(8,128)(2,1)}), bf16[8,8,4096]{2,1,0:T(8,128)(2,1)S(1)}, u32[]{:S(2)}, u32[]{:S(2)}) %all-to-all-start) | async-done | bytes 524320 | tf_op jit(solution)/shard_map/all_to_all | solution.py:47
  28.9 10.9 %collective-permute-start.2 = (bf16[64,4096]{1,0:T(8,128)(2,1)S(1)}, bf16[64,4096]{1,0:T(8,128)(2,1)S(1)}, u32[]{:S(2)}, u32[]{:S(2)}) collective-permute-start(bf16[64,4096]{1,0:T(8,128)(2,1)S(1)} %bitcast.131), channel_id=1, source_target_pairs={{0,56},{8,0},{16,8},{24,16},{32,24},{40,32},{48,40},{56,48},{1,57}... | collective-permute-start | bytes 1572872 | tf_op jit(solution)/shard_map/ppermute | solution.py:54
  39.9 1.9 %collective-permute-start.1 = (bf16[64,4096]{1,0:T(8,128)(2,1)S(1)}, bf16[64,4096]{1,0:T(8,128)(2,1)S(1)}, u32[]{:S(2)}, u32[]{:S(2)}) collective-permute-start(bf16[64,4096]{1,0:T(8,128)(2,1)S(1)} %bitcast.132), channel_id=1, source_target_pairs={{0,8},{8,16},{16,24},{24,32},{32,40},{40,48},{48,56},{56,0},{1,9},... | collective-permute-start | bytes 1572872 | tf_op jit(solution)/shard_map/ppermute | solution.py:54
  41.8 1.8 %pad_maximum_fusion = bf16[4096,256]{1,0:T(8,128)(2,1)S(1)} fusion(bf16[4096,128]{1,0:T(8,128)(2,1)} %collective-permute-done.10, bf16[4096,128]{1,0:T(8,128)(2,1)} %constant_dynamic-slice_fusion), kind=kLoop, calls=%fused_computation.17 | loop fusion | flops 4194304 | bytes 4194304 | tf_op jit(solution)/shard_map/concatenate | solution.py:141
  44.4 2.2 %collective-permute-done.2 = bf16[64,4096]{1,0:T(8,128)(2,1)S(1)} collective-permute-done((bf16[64,4096]{1,0:T(8,128)(2,1)S(1)}, bf16[64,4096]{1,0:T(8,128)(2,1)S(1)}, u32[]{:S(2)}, u32[]{:S(2)}) %collective-permute-start.2) | collective-permute-done | bytes 524320 | tf_op jit(solution)/shard_map/ppermute | solution.py:54
  46.5 5.6 %collective-permute-start.4 = (bf16[64,4096]{1,0:T(8,128)(2,1)S(1)}, bf16[64,4096]{1,0:T(8,128)(2,1)S(1)}, u32[]{:S(2)}, u32[]{:S(2)}) collective-permute-start(bf16[64,4096]{1,0:T(8,128)(2,1)S(1)} %collective-permute-done.2), channel_id=1, source_target_pairs={{0,56},{8,0},{16,8},{24,16},{32,24},{40,32},{48,40},{56,48},{1,57}... | collective-permute-start | bytes 1572872 | tf_op jit(solution)/shard_map/ppermute | solution.py:54
  52.2 1.9 %collective-permute-start.3 = (bf16[64,4096]{1,0:T(8,128)(2,1)S(1)}, bf16[64,4096]{1,0:T(8,128)(2,1)S(1)}, u32[]{:S(2)}, u32[]{:S(2)}) collective-permute-start(bf16[64,4096]{1,0:T(8,128)(2,1)S(1)} %collective-permute-done.1), channel_id=1, source_target_pairs={{0,8},{8,16},{16,24},{24,32},{32,40},{40,48},{48,56},{56,0},{1,9},... | collective-permute-start | bytes 1572872 | tf_op jit(solution)/shard_map/ppermute | solution.py:54
  55.1 3.7 %collective-permute-done.4 = bf16[64,4096]{1,0:T(8,128)(2,1)S(1)} collective-permute-done((bf16[64,4096]{1,0:T(8,128)(2,1)S(1)}, bf16[64,4096]{1,0:T(8,128)(2,1)S(1)}, u32[]{:S(2)}, u32[]{:S(2)}) %collective-permute-start.4) | collective-permute-done | bytes 524320 | tf_op jit(solution)/shard_map/ppermute | solution.py:54
  58.8 5.6 %collective-permute-start.6 = (bf16[64,4096]{1,0:T(8,128)(2,1)S(1)}, bf16[64,4096]{1,0:T(8,128)(2,1)S(1)}, u32[]{:S(2)}, u32[]{:S(2)}) collective-permute-start(bf16[64,4096]{1,0:T(8,128)(2,1)S(1)} %collective-permute-done.4), channel_id=1, source_target_pairs={{0,56},{8,0},{16,8},{24,16},{32,24},{40,32},{48,40},{56,48},{1,57}... | collective-permute-start | bytes 1572872 | tf_op jit(solution)/shard_map/ppermute | solution.py:54
  64.4 1.9 %collective-permute-start.5 = (bf16[64,4096]{1,0:T(8,128)(2,1)S(1)}, bf16[64,4096]{1,0:T(8,128)(2,1)S(1)}, u32[]{:S(2)}, u32[]{:S(2)}) collective-permute-start(bf16[64,4096]{1,0:T(8,128)(2,1)S(1)} %collective-permute-done.3), channel_id=1, source_target_pairs={{0,8},{8,16},{16,24},{24,32},{32,40},{40,48},{48,56},{56,0},{1,9},... | collective-permute-start | bytes 1572872 | tf_op jit(solution)/shard_map/ppermute | solution.py:54
  67.4 3.7 %collective-permute-done.6 = bf16[64,4096]{1,0:T(8,128)(2,1)S(1)} collective-permute-done((bf16[64,4096]{1,0:T(8,128)(2,1)S(1)}, bf16[64,4096]{1,0:T(8,128)(2,1)S(1)}, u32[]{:S(2)}, u32[]{:S(2)}) %collective-permute-start.6) | collective-permute-done | bytes 524320 | tf_op jit(solution)/shard_map/ppermute | solution.py:54
  71.1 5.6 %collective-permute-start.8 = (bf16[64,2048]{1,0:T(8,128)(2,1)S(1)}, bf16[64,2048]{1,0:T(8,128)(2,1)S(1)}, u32[]{:S(2)}, u32[]{:S(2)}) collective-permute-start(bf16[64,2048]{1,0:T(8,128)(2,1)S(1)} %slice.109), channel_id=1, source_target_pairs={{0,56},{8,0},{16,8},{24,16},{32,24},{40,32},{48,40},{56,48},{1,57}... | collective-permute-start | bytes 786440 | tf_op jit(solution)/shard_map/ppermute | solution.py:54
  76.8 1.9 %collective-permute-start.7 = (bf16[64,2048]{1,0:T(8,128)(2,1)S(1)}, bf16[64,2048]{1,0:T(8,128)(2,1)S(1)}, u32[]{:S(2)}, u32[]{:S(2)}) collective-permute-start(bf16[64,2048]{1,0:T(8,128)(2,1)S(1)} %slice.108), channel_id=1, source_target_pairs={{0,8},{8,16},{16,24},{24,32},{32,40},{40,48},{48,56},{56,0},{1,9},... | collective-permute-start | bytes 786440 | tf_op jit(solution)/shard_map/ppermute | solution.py:54
  80.8 5.4 %collective-permute-done.7 = bf16[64,2048]{1,0:T(8,128)(2,1)S(1)} collective-permute-done((bf16[64,2048]{1,0:T(8,128)(2,1)S(1)}, bf16[64,2048]{1,0:T(8,128)(2,1)S(1)}, u32[]{:S(2)}, u32[]{:S(2)}) %collective-permute-start.7) | collective-permute-done | bytes 262176 | tf_op jit(solution)/shard_map/ppermute | solution.py:54
  86.9 2.6 %collective-permute-start.9 = (bf16[32,4096]{1,0:T(8,128)(2,1)S(1)}, bf16[32,4096]{1,0:T(8,128)(2,1)S(1)}, u32[]{:S(2)}, u32[]{:S(2)}) collective-permute-start(bf16[32,4096]{1,0:T(8,128)(2,1)S(1)} %get-tuple-element.13), channel_id=1, source_target_pairs={{0,1},{1,0},{2,3},{3,2},{4,5},{5,4},{6,7},{7,6},{8,9},{9,8},{10,11... | collective-permute-start | bytes 786440 | tf_op jit(solution)/shard_map/ppermute | solution.py:59
  91.6 3.6 %collective-permute-done.9.theirs_ref = bf16[32,4096]{1,0:T(8,128)(2,1)S(1)} collective-permute-done((bf16[32,4096]{1,0:T(8,128)(2,1)S(1)}, bf16[32,4096]{1,0:T(8,128)(2,1)S(1)}, u32[]{:S(2)}, u32[]{:S(2)}) %collective-permute-start.9) | collective-permute-done | bytes 262176 | tf_op jit(solution)/shard_map/ppermute | solution.py:59
  96.3 5.5 %all-to-all-start.1 = ((bf16[64,16,128]{2,1,0:T(8,128)(2,1)}), bf16[64,16,128]{2,1,0:T(8,128)(2,1)S(1)}, u32[]{:S(2)}, u32[]{:S(2)}) async-start(bf16[64,16,128]{2,1,0:T(8,128)(2,1)} %shard_map.82), calls=%async_computation.1 | async-start | bytes 524288 | tf_op jit(solution)/shard_map/all_to_all | solution.py:197
  102.0 3.5 %collective-permute-start.11 = (f32[512,128]{1,0:T(8,128)S(1)}, f32[512,128]{1,0:T(8,128)S(1)}, u32[]{:S(2)}, u32[]{:S(2)}) collective-permute-start(f32[512,128]{1,0:T(8,128)S(1)} %slice.92), channel_id=1, source_target_pairs={{0,1},{1,0},{2,3},{3,2},{4,5},{5,4},{6,7},{7,6},{8,9},{9,8},{10,11... | collective-permute-start | bytes 786440 | tf_op jit(solution)/shard_map/ppermute | solution.py:59
  105.5 10.0 %all-to-all-done.1 = bf16[64,16,128]{2,1,0:T(8,128)(2,1)S(1)} async-done(((bf16[64,16,128]{2,1,0:T(8,128)(2,1)}), bf16[64,16,128]{2,1,0:T(8,128)(2,1)S(1)}, u32[]{:S(2)}, u32[]{:S(2)}) %all-to-all-start.1) | async-done | bytes 262176 | tf_op jit(solution)/shard_map/all_to_all | solution.py:197
  119.4 5.6 %all-to-all-start.2 = ((bf16[64,8,128]{2,1,0:T(8,128)(2,1)}), bf16[64,8,128]{2,1,0:T(8,128)(2,1)S(1)}, u32[]{:S(2)}, u32[]{:S(2)}) async-start(bf16[64,8,128]{2,1,0:T(8,128)(2,1)} %bitcast.24), calls=%async_computation.2 | async-start | bytes 262144 | tf_op jit(solution)/shard_map/all_to_all | solution.py:220
  126.0 11.7 %all-to-all-done.2 = bf16[64,8,128]{2,1,0:T(8,128)(2,1)S(1)} async-done(((bf16[64,8,128]{2,1,0:T(8,128)(2,1)}), bf16[64,8,128]{2,1,0:T(8,128)(2,1)S(1)}, u32[]{:S(2)}, u32[]{:S(2)}) %all-to-all-start.2) | async-done | bytes 131104 | tf_op jit(solution)/shard_map/all_to_all | solution.py:220
  (88 shorter events, 21.8 us)
Async XLA Ops:
  0.0 1.6 %copy-start = (bf16[1,8192,128]{2,1,0:T(8,128)(2,1)S(1)}, bf16[1,8192,128]{2,1,0:T(8,128)(2,1)}, u32[]{:S(2)}) copy-start(bf16[1,8192,128]{2,1,0:T(8,128)(2,1)} %param.10) | copy-start | bytes 6291460
  0.0 6.4 %copy-start.4 = (f32[1,8192]{1,0:T(1,128)S(1)}, f32[1,8192]{1,0:T(1,128)}, u32[]{:S(2)}) copy-start(f32[1,8192]{1,0:T(1,128)} %param.9) | copy-start | bytes 98308
  0.0 6.2 %collective-permute-start = (bf16[8,8192]{1,0:T(8,128)(2,1)}, bf16[8,8192]{1,0:T(8,128)(2,1)S(1)}, u32[]{:S(2)}, u32[]{:S(2)}) collective-permute-start(bf16[8,8192]{1,0:T(8,128)(2,1)} %param.8), channel_id=1, source_target_pairs={{0,64},{64,128},{128,192},{192,256},{256,320},{320,384},{384,448},... | collective-permute-start | bytes 393224 | tf_op jit(solution)/shard_map/ppermute | solution.py:37
  1.6 12.0 %copy-start.5 = (s32[512]{0:T(512)S(1)}, s32[512]{0:T(512)}, u32[]{:S(2)}) copy-start(s32[512]{0:T(512)} %param.13) | copy-start | bytes 6148
  2.6 39.2 %collective-permute-start.10 = (bf16[4096,128]{1,0:T(8,128)(2,1)}, bf16[4096,128]{1,0:T(8,128)(2,1)}, u32[]{:S(2)}, u32[]{:S(2)}) collective-permute-start(bf16[4096,128]{1,0:T(8,128)(2,1)} %dynamic-slice_bitcast_fusion), channel_id=1, source_target_pairs={{0,1},{1,0},{2,3},{3,2},{4,5},{5,4},{6,7},{7,6},{8,9},{9,8},{10,11... | collective-permute-start | bytes 3145736 | tf_op jit(solution)/shard_map/ppermute | solution.py:59
  7.4 21.6 %all-to-all-start = ((bf16[8,8,4096]{2,1,0:T(8,128)(2,1)}), bf16[8,8,4096]{2,1,0:T(8,128)(2,1)S(1)}, u32[]{:S(2)}, u32[]{:S(2)}) async-start(bf16[8,8,4096]{2,1,0:T(8,128)(2,1)} %bitcast.12), calls=%async_computation | async-start | bytes 1048576 | tf_op jit(solution)/shard_map/all_to_all | solution.py:47
  28.9 17.6 %collective-permute-start.2 = (bf16[64,4096]{1,0:T(8,128)(2,1)S(1)}, bf16[64,4096]{1,0:T(8,128)(2,1)S(1)}, u32[]{:S(2)}, u32[]{:S(2)}) collective-permute-start(bf16[64,4096]{1,0:T(8,128)(2,1)S(1)} %bitcast.131), channel_id=1, source_target_pairs={{0,56},{8,0},{16,8},{24,16},{32,24},{40,32},{48,40},{56,48},{1,57}... | collective-permute-start | bytes 1572872 | tf_op jit(solution)/shard_map/ppermute | solution.py:54
  39.9 12.3 %collective-permute-start.1 = (bf16[64,4096]{1,0:T(8,128)(2,1)S(1)}, bf16[64,4096]{1,0:T(8,128)(2,1)S(1)}, u32[]{:S(2)}, u32[]{:S(2)}) collective-permute-start(bf16[64,4096]{1,0:T(8,128)(2,1)S(1)} %bitcast.132), channel_id=1, source_target_pairs={{0,8},{8,16},{16,24},{24,32},{32,40},{40,48},{48,56},{56,0},{1,9},... | collective-permute-start | bytes 1572872 | tf_op jit(solution)/shard_map/ppermute | solution.py:54
  46.5 12.3 %collective-permute-start.4 = (bf16[64,4096]{1,0:T(8,128)(2,1)S(1)}, bf16[64,4096]{1,0:T(8,128)(2,1)S(1)}, u32[]{:S(2)}, u32[]{:S(2)}) collective-permute-start(bf16[64,4096]{1,0:T(8,128)(2,1)S(1)} %collective-permute-done.2), channel_id=1, source_target_pairs={{0,56},{8,0},{16,8},{24,16},{32,24},{40,32},{48,40},{56,48},{1,57}... | collective-permute-start | bytes 1572872 | tf_op jit(solution)/shard_map/ppermute | solution.py:54
  52.2 12.3 %collective-permute-start.3 = (bf16[64,4096]{1,0:T(8,128)(2,1)S(1)}, bf16[64,4096]{1,0:T(8,128)(2,1)S(1)}, u32[]{:S(2)}, u32[]{:S(2)}) collective-permute-start(bf16[64,4096]{1,0:T(8,128)(2,1)S(1)} %collective-permute-done.1), channel_id=1, source_target_pairs={{0,8},{8,16},{16,24},{24,32},{32,40},{40,48},{48,56},{56,0},{1,9},... | collective-permute-start | bytes 1572872 | tf_op jit(solution)/shard_map/ppermute | solution.py:54
  58.8 12.3 %collective-permute-start.6 = (bf16[64,4096]{1,0:T(8,128)(2,1)S(1)}, bf16[64,4096]{1,0:T(8,128)(2,1)S(1)}, u32[]{:S(2)}, u32[]{:S(2)}) collective-permute-start(bf16[64,4096]{1,0:T(8,128)(2,1)S(1)} %collective-permute-done.4), channel_id=1, source_target_pairs={{0,56},{8,0},{16,8},{24,16},{32,24},{40,32},{48,40},{56,48},{1,57}... | collective-permute-start | bytes 1572872 | tf_op jit(solution)/shard_map/ppermute | solution.py:54
  64.4 12.3 %collective-permute-start.5 = (bf16[64,4096]{1,0:T(8,128)(2,1)S(1)}, bf16[64,4096]{1,0:T(8,128)(2,1)S(1)}, u32[]{:S(2)}, u32[]{:S(2)}) collective-permute-start(bf16[64,4096]{1,0:T(8,128)(2,1)S(1)} %collective-permute-done.3), channel_id=1, source_target_pairs={{0,8},{8,16},{16,24},{24,32},{32,40},{40,48},{48,56},{56,0},{1,9},... | collective-permute-start | bytes 1572872 | tf_op jit(solution)/shard_map/ppermute | solution.py:54
  71.1 9.5 %collective-permute-start.8 = (bf16[64,2048]{1,0:T(8,128)(2,1)S(1)}, bf16[64,2048]{1,0:T(8,128)(2,1)S(1)}, u32[]{:S(2)}, u32[]{:S(2)}) collective-permute-start(bf16[64,2048]{1,0:T(8,128)(2,1)S(1)} %slice.109), channel_id=1, source_target_pairs={{0,56},{8,0},{16,8},{24,16},{32,24},{40,32},{48,40},{56,48},{1,57}... | collective-permute-start | bytes 786440 | tf_op jit(solution)/shard_map/ppermute | solution.py:54
  76.8 9.5 %collective-permute-start.7 = (bf16[64,2048]{1,0:T(8,128)(2,1)S(1)}, bf16[64,2048]{1,0:T(8,128)(2,1)S(1)}, u32[]{:S(2)}, u32[]{:S(2)}) collective-permute-start(bf16[64,2048]{1,0:T(8,128)(2,1)S(1)} %slice.108), channel_id=1, source_target_pairs={{0,8},{8,16},{16,24},{24,32},{32,40},{40,48},{48,56},{56,0},{1,9},... | collective-permute-start | bytes 786440 | tf_op jit(solution)/shard_map/ppermute | solution.py:54
  86.9 8.3 %collective-permute-start.9 = (bf16[32,4096]{1,0:T(8,128)(2,1)S(1)}, bf16[32,4096]{1,0:T(8,128)(2,1)S(1)}, u32[]{:S(2)}, u32[]{:S(2)}) collective-permute-start(bf16[32,4096]{1,0:T(8,128)(2,1)S(1)} %get-tuple-element.13), channel_id=1, source_target_pairs={{0,1},{1,0},{2,3},{3,2},{4,5},{5,4},{6,7},{7,6},{8,9},{9,8},{10,11... | collective-permute-start | bytes 786440 | tf_op jit(solution)/shard_map/ppermute | solution.py:59
  90.6 4.5 %copy-start.1 = (bf16[1,1,8192,64]{2,3,1,0:T(8,128)(2,1)S(1)}, bf16[1,1,8192,64]{2,3,1,0:T(8,128)(2,1)}, u32[]{:S(2)}) copy-start(bf16[1,1,8192,64]{2,3,1,0:T(8,128)(2,1)} %param.11) | copy-start | bytes 3145732
  96.3 19.1 %all-to-all-start.1 = ((bf16[64,16,128]{2,1,0:T(8,128)(2,1)}), bf16[64,16,128]{2,1,0:T(8,128)(2,1)S(1)}, u32[]{:S(2)}, u32[]{:S(2)}) async-start(bf16[64,16,128]{2,1,0:T(8,128)(2,1)} %shard_map.82), calls=%async_computation.1 | async-start | bytes 524288 | tf_op jit(solution)/shard_map/all_to_all | solution.py:197
  102.0 14.5 %collective-permute-start.11 = (f32[512,128]{1,0:T(8,128)S(1)}, f32[512,128]{1,0:T(8,128)S(1)}, u32[]{:S(2)}, u32[]{:S(2)}) collective-permute-start(f32[512,128]{1,0:T(8,128)S(1)} %slice.92), channel_id=1, source_target_pairs={{0,1},{1,0},{2,3},{3,2},{4,5},{5,4},{6,7},{7,6},{8,9},{9,8},{10,11... | collective-permute-start | bytes 786440 | tf_op jit(solution)/shard_map/ppermute | solution.py:59
  116.1 1.2 copy-start.2
  117.4 7.6 %copy-start.3 = (bf16[8,2,16,1024]{3,2,1,0:T(8,128)(2,1)S(1)}, bf16[8,2,16,1024]{3,2,1,0:T(8,128)(2,1)}, u32[]{:S(2)}) copy-start(bf16[8,2,16,1024]{3,2,1,0:T(8,128)(2,1)} %param.15) | copy-start | bytes 1572868
  119.4 18.3 %all-to-all-start.2 = ((bf16[64,8,128]{2,1,0:T(8,128)(2,1)}), bf16[64,8,128]{2,1,0:T(8,128)(2,1)S(1)}, u32[]{:S(2)}, u32[]{:S(2)}) async-start(bf16[64,8,128]{2,1,0:T(8,128)(2,1)} %bitcast.24), calls=%async_computation.2 | async-start | bytes 262144 | tf_op jit(solution)/shard_map/all_to_all | solution.py:220

commit v3 on v2

--- a/solution.py
+++ b/solution.py
@@ -147,33 +147,34 @@
     blocks = [None] * SIDE
     blocks[0] = ahead = behind = line
     for step in range(1, SIDE // 2):
+        if step == 3:
+            low_piece, high_piece = ahead[:, :quarter], behind[:, quarter:]
         ahead = along_line(ahead, lines_a, 1)
         behind = along_line(behind, lines_a, -1)
         blocks[SIDE - step], blocks[step] = ahead, behind
-    far_low = along_line(ahead[:, :quarter], lines_a, 1)
-    far_high = along_line(behind[:, quarter:], lines_a, -1)
+    far_low = along_line(low_piece, lines_a, 2)
+    far_high = along_line(high_piece, lines_a, -2)
 
     adapters = jnp.arange(bank, dtype=jnp.int32)[None, :]
     named = request_adapter_index[:, None] == adapters
     counts = jnp.cumsum(named.astype(jnp.int32), axis=0)
     slot = jnp.sum(jnp.where(named, counts, 0), axis=1) - 1
-    both = jnp.stack([request_adapter_index, slot], axis=1)
-    both = swap_sides(odd, both).reshape(SIDE, line_rows, 2)
-    both = jnp.roll(both, -at_a, axis=0).reshape(segment_rows, 2)
-    index, slot = both[:, 0], both[:, 1]
-    hot = index[:, None] == adapters
+    some = OWN_MAX // 2
+    place = (
+        (request_adapter_index * some + slot % some)[:, None]
+        == jnp.arange(bank * some, dtype=jnp.int32)[None, :]
+    ).astype(jnp.bfloat16)
+    lower = (slot < some)[:, None]
+    turned = jnp.stack([request_adapter_index, slot], axis=1)
+    turned = swap_sides(odd, turned).reshape(SIDE, line_rows, 2)
+    turned = jnp.roll(turned, -at_a, axis=0).reshape(segment_rows, 2)
+    index, turned_slot = turned[:, 0], turned[:, 1]
     partner = jnp.where(odd, position + SIDE * (1 - 2 * which), position + (1 - 2 * which))
     owners = jnp.stack([position, partner])
     pick = (
-        (jnp.arange(OWN_MAX, dtype=jnp.int32)[None, :, None] == slot[None, None, :])
+        (jnp.arange(OWN_MAX, dtype=jnp.int32)[None, :, None] == turned_slot[None, None, :])
         & (index[None, None, :] == owners[:, None, None])
     ).astype(jnp.bfloat16).reshape(2 * OWN_MAX, SIDE, line_rows)
-    some = OWN_MAX // 2
-    place = (
-        (index * some + slot % some)[:, None]
-        == jnp.arange(bank * some, dtype=jnp.int32)[None, :]
-    ).astype(jnp.bfloat16)
-
     def pick_from(j, block):
         return jnp.dot(pick[:, j], block, preferred_element_type=jnp.float32).astype(jnp.bfloat16)
 
@@ -194,6 +195,8 @@
     products[far] = times(far_low, 0, quarter) + times(far_high, quarter, half)
     product = jnp.concatenate(products, axis=0)
     shrunk, product = lax.optimization_barrier((shrunk, product))
+    product = jnp.roll(product.reshape(SIDE, line_rows, -1), at_a, axis=0)
+    product = swap_sides(odd, product.reshape(segment_rows, -1))
     slots = lax.all_to_all(
         shrunk,
         "adapter",
@@ -204,8 +207,8 @@
 
     base_query = product[:, :column_list] + to_partner(product[:, column_list:], lines_b)
     both = jnp.dot(place, slots, preferred_element_type=jnp.float32).astype(jnp.bfloat16)
-    shrunk_tok = jnp.where((slot < some)[:, None], both[:, :rank_width], both[:, rank_width:])
-    spread = (hot.astype(jnp.bfloat16)[:, :, None] * shrunk_tok[:, None, :]).reshape(
+    shrunk_tok = jnp.where(lower, both[:, :rank_width], both[:, rank_width:])
+    spread = (named.astype(jnp.bfloat16)[:, :, None] * shrunk_tok[:, None, :]).reshape(
         segment_rows, bank * rank_width
     )
     adapter_update = jnp.dot(
@@ -214,9 +217,6 @@
         preferred_element_type=jnp.float32,
     )
     query_rows = (base_query + adapter_scale * adapter_update).astype(jnp.bfloat16)
-    query_rows = query_rows.reshape(SIDE, line_rows, column_list)
-    query_rows = jnp.roll(query_rows, at_a, axis=0)
-    query_rows = swap_sides(odd, query_rows.reshape(segment_rows, column_list))
     own_queries = lax.all_to_all(
         query_rows.reshape(HEADS, tok_dev, HD), "adapter", split_axis=0, concat_axis=0, tiled=True
     )

time: 141 us -> 140 us (level)
  transfers between devices with their start and end apart: 15 -> 15, of which waited for: 9 -> 10; matrix products, arithmetic and copies ran while one was open for 11% -> 11% of each run, Pallas kernels for 0% -> 0%
where the time goes in v3:
time: 140 us; the launch traced here: 139 us
  starting transfers between devices  61.7 us (44%)
  waiting for transfers between devices  52.5 us (38%)
  matrix products  10.3 us (7%)
  local copies, waits for them, and re-layouts  8.12 us (6%)
  other arithmetic  4.39 us (3%)
    ppermute x8, starting transfers between devices, along_line(): return lax.ppermute(block, BOTH, pairs)  34.1 us
    ppermute x8, waiting for transfers between devices, along_line(): return lax.ppermute(block, BOTH, pairs)  15.9 us
    all_to_all x1, waiting for transfers between devices, body(): lax.all_to_all(query_rows.reshape(HEADS, tok_dev, HD), 'adapter', split_a...  11.7 us
    all_to_all x1, waiting for transfers between devices, over_line(): lax.all_to_all(blocks, BOTH, split_axis=0, concat_axis=0, tiled=True, axi...  11.6 us
    all_to_all x1, waiting for transfers between devices, body(): lax.all_to_all(shrunk, 'adapter', split_axis=0, concat_axis=0, tiled=True)  9.93 us
    ppermute x3, starting transfers between devices, to_partner(): return lax.ppermute(block, BOTH, pairs)  9.57 us
    all_to_all x1, starting transfers between devices, over_line(): lax.all_to_all(blocks, BOTH, split_axis=0, concat_axis=0, tiled=True, axi...  6.2 us
    all_to_all x1, starting transfers between devices, body(): lax.all_to_all(shrunk, 'adapter', split_axis=0, concat_axis=0, tiled=True)  6.14 us
  transfers between devices with their start and end apart: 15, of which 10 were waited for; matrix products, arithmetic and copies ran while one was open for 11% of the time, Pallas kernels for 0%

profile of v3, /device:TPU:2, one launch (start us, length us, event | category | flops | bytes accessed | tf_op | source)
XLA Modules:
  0.0 138.8 jit_solution(8208780020793080458)
XLA Ops:
  2.6 3.5 %collective-permute-start.10 = (bf16[4096,128]{1,0:T(8,128)(2,1)}, bf16[4096,128]{1,0:T(8,128)(2,1)}, u32[]{:S(2)}, u32[]{:S(2)}) collective-permute-start(bf16[4096,128]{1,0:T(8,128)(2,1)} %dynamic-slice_bitcast_fusion), channel_id=1, source_target_pairs={{0,1},{1,0},{2,3},{3,2},{4,5},{5,4},{6,7},{7,6},{8,9},{9,8},{10,11... | collective-permute-start | bytes 3145736 | tf_op jit(solution)/shard_map/ppermute | solution.py:59
  7.4 6.2 %all-to-all-start = ((bf16[8,8,4096]{2,1,0:T(8,128)(2,1)}), bf16[8,8,4096]{2,1,0:T(8,128)(2,1)S(1)}, u32[]{:S(2)}, u32[]{:S(2)}) async-start(bf16[8,8,4096]{2,1,0:T(8,128)(2,1)} %bitcast.12), calls=%async_computation | async-start | bytes 1048576 | tf_op jit(solution)/shard_map/all_to_all | solution.py:47
  17.3 11.6 %all-to-all-done = bf16[8,8,4096]{2,1,0:T(8,128)(2,1)S(1)} async-done(((bf16[8,8,4096]{2,1,0:T(8,128)(2,1)}), bf16[8,8,4096]{2,1,0:T(8,128)(2,1)S(1)}, u32[]{:S(2)}, u32[]{:S(2)}) %all-to-all-start) | async-done | bytes 524320 | tf_op jit(solution)/shard_map/all_to_all | solution.py:47
  28.9 10.9 %collective-permute-start.2 = (bf16[64,4096]{1,0:T(8,128)(2,1)S(1)}, bf16[64,4096]{1,0:T(8,128)(2,1)S(1)}, u32[]{:S(2)}, u32[]{:S(2)}) collective-permute-start(bf16[64,4096]{1,0:T(8,128)(2,1)S(1)} %bitcast.134), channel_id=1, source_target_pairs={{0,56},{8,0},{16,8},{24,16},{32,24},{40,32},{48,40},{56,48},{1,57}... | collective-permute-start | bytes 1572872 | tf_op jit(solution)/shard_map/ppermute | solution.py:54
  39.9 1.9 %collective-permute-start.1 = (bf16[64,4096]{1,0:T(8,128)(2,1)S(1)}, bf16[64,4096]{1,0:T(8,128)(2,1)S(1)}, u32[]{:S(2)}, u32[]{:S(2)}) collective-permute-start(bf16[64,4096]{1,0:T(8,128)(2,1)S(1)} %bitcast.135), channel_id=1, source_target_pairs={{0,8},{8,16},{16,24},{24,32},{32,40},{40,48},{48,56},{56,0},{1,9},... | collective-permute-start | bytes 1572872 | tf_op jit(solution)/shard_map/ppermute | solution.py:54
  41.8 1.8 %pad_maximum_fusion = bf16[4096,256]{1,0:T(8,128)(2,1)S(1)} fusion(bf16[4096,128]{1,0:T(8,128)(2,1)} %collective-permute-done.10, bf16[4096,128]{1,0:T(8,128)(2,1)} %constant_dynamic-slice_fusion), kind=kLoop, calls=%fused_computation.17 | loop fusion | flops 4194304 | bytes 4194304 | tf_op jit(solution)/shard_map/concatenate | solution.py:141
  44.3 2.2 %collective-permute-done.2 = bf16[64,4096]{1,0:T(8,128)(2,1)S(1)} collective-permute-done((bf16[64,4096]{1,0:T(8,128)(2,1)S(1)}, bf16[64,4096]{1,0:T(8,128)(2,1)S(1)}, u32[]{:S(2)}, u32[]{:S(2)}) %collective-permute-start.2) | collective-permute-done | bytes 524320 | tf_op jit(solution)/shard_map/ppermute | solution.py:54
  46.5 5.6 %collective-permute-start.4 = (bf16[64,4096]{1,0:T(8,128)(2,1)S(1)}, bf16[64,4096]{1,0:T(8,128)(2,1)S(1)}, u32[]{:S(2)}, u32[]{:S(2)}) collective-permute-start(bf16[64,4096]{1,0:T(8,128)(2,1)S(1)} %collective-permute-done.2), channel_id=1, source_target_pairs={{0,56},{8,0},{16,8},{24,16},{32,24},{40,32},{48,40},{56,48},{1,57}... | collective-permute-start | bytes 1572872 | tf_op jit(solution)/shard_map/ppermute | solution.py:54
  52.2 1.9 %collective-permute-start.3 = (bf16[64,4096]{1,0:T(8,128)(2,1)S(1)}, bf16[64,4096]{1,0:T(8,128)(2,1)S(1)}, u32[]{:S(2)}, u32[]{:S(2)}) collective-permute-start(bf16[64,4096]{1,0:T(8,128)(2,1)S(1)} %collective-permute-done.1), channel_id=1, source_target_pairs={{0,8},{8,16},{16,24},{24,32},{32,40},{40,48},{48,56},{56,0},{1,9},... | collective-permute-start | bytes 1572872 | tf_op jit(solution)/shard_map/ppermute | solution.py:54
  55.1 3.7 %collective-permute-done.4 = bf16[64,4096]{1,0:T(8,128)(2,1)S(1)} collective-permute-done((bf16[64,4096]{1,0:T(8,128)(2,1)S(1)}, bf16[64,4096]{1,0:T(8,128)(2,1)S(1)}, u32[]{:S(2)}, u32[]{:S(2)}) %collective-permute-start.4) | collective-permute-done | bytes 524320 | tf_op jit(solution)/shard_map/ppermute | solution.py:54
  58.8 3.8 %collective-permute-start.8 = (bf16[64,2048]{1,0:T(8,128)(2,1)S(1)}, bf16[64,2048]{1,0:T(8,128)(2,1)S(1)}, u32[]{:S(2)}, u32[]{:S(2)}) collective-permute-start(bf16[64,2048]{1,0:T(8,128)(2,1)S(1)} %slice.109), channel_id=1, source_target_pairs={{0,48},{8,56},{16,0},{24,8},{32,16},{40,24},{48,32},{56,40},{1,49}... | collective-permute-start | bytes 786440 | tf_op jit(solution)/shard_map/ppermute | solution.py:54
  62.7 1.7 %collective-permute-done.3 = bf16[64,4096]{1,0:T(8,128)(2,1)S(1)} collective-permute-done((bf16[64,4096]{1,0:T(8,128)(2,1)S(1)}, bf16[64,4096]{1,0:T(8,128)(2,1)S(1)}, u32[]{:S(2)}, u32[]{:S(2)}) %collective-permute-start.3) | collective-permute-done | bytes 524320 | tf_op jit(solution)/shard_map/ppermute | solution.py:54
  64.5 1.9 %collective-permute-start.7 = (bf16[64,2048]{1,0:T(8,128)(2,1)S(1)}, bf16[64,2048]{1,0:T(8,128)(2,1)S(1)}, u32[]{:S(2)}, u32[]{:S(2)}) collective-permute-start(bf16[64,2048]{1,0:T(8,128)(2,1)S(1)} %slice.108), channel_id=1, source_target_pairs={{0,16},{8,24},{16,32},{24,40},{32,48},{40,56},{48,0},{56,8},{1,17}... | collective-permute-start | bytes 786440 | tf_op jit(solution)/shard_map/ppermute | solution.py:54
  66.4 6.1 %collective-permute-start.6 = (bf16[64,4096]{1,0:T(8,128)(2,1)S(1)}, bf16[64,4096]{1,0:T(8,128)(2,1)S(1)}, u32[]{:S(2)}, u32[]{:S(2)}) collective-permute-start(bf16[64,4096]{1,0:T(8,128)(2,1)S(1)} %collective-permute-done.4), channel_id=1, source_target_pairs={{0,56},{8,0},{16,8},{24,16},{32,24},{40,32},{48,40},{56,48},{1,57}... | collective-permute-start | bytes 1572872 | tf_op jit(solution)/shard_map/ppermute | solution.py:54
  72.5 1.9 %collective-permute-start.5 = (bf16[64,4096]{1,0:T(8,128)(2,1)S(1)}, bf16[64,4096]{1,0:T(8,128)(2,1)S(1)}, u32[]{:S(2)}, u32[]{:S(2)}) collective-permute-start(bf16[64,4096]{1,0:T(8,128)(2,1)S(1)} %collective-permute-done.3), channel_id=1, source_target_pairs={{0,8},{8,16},{16,24},{24,32},{32,40},{40,48},{48,56},{56,0},{1,9},... | collective-permute-start | bytes 1572872 | tf_op jit(solution)/shard_map/ppermute | solution.py:54
  79.4 5.3 %collective-permute-done.5 = bf16[64,4096]{1,0:T(8,128)(2,1)S(1)} collective-permute-done((bf16[64,4096]{1,0:T(8,128)(2,1)S(1)}, bf16[64,4096]{1,0:T(8,128)(2,1)S(1)}, u32[]{:S(2)}, u32[]{:S(2)}) %collective-permute-start.5) | collective-permute-done | bytes 524320 | tf_op jit(solution)/shard_map/ppermute | solution.py:54
  85.2 2.6 %collective-permute-start.9 = (bf16[32,4096]{1,0:T(8,128)(2,1)S(1)}, bf16[32,4096]{1,0:T(8,128)(2,1)S(1)}, u32[]{:S(2)}, u32[]{:S(2)}) collective-permute-start(bf16[32,4096]{1,0:T(8,128)(2,1)S(1)} %get-tuple-element.13), channel_id=1, source_target_pairs={{0,1},{1,0},{2,3},{3,2},{4,5},{5,4},{6,7},{7,6},{8,9},{9,8},{10,11... | collective-permute-start | bytes 786440 | tf_op jit(solution)/shard_map/ppermute | solution.py:59
  90.0 3.4 %collective-permute-done.9.theirs_ref = bf16[32,4096]{1,0:T(8,128)(2,1)S(1)} collective-permute-done((bf16[32,4096]{1,0:T(8,128)(2,1)S(1)}, bf16[32,4096]{1,0:T(8,128)(2,1)S(1)}, u32[]{:S(2)}, u32[]{:S(2)}) %collective-permute-start.9) | collective-permute-done | bytes 262176 | tf_op jit(solution)/shard_map/ppermute | solution.py:59
  94.6 6.1 %all-to-all-start.1 = ((bf16[64,16,128]{2,1,0:T(8,128)(2,1)}), bf16[64,16,128]{2,1,0:T(8,128)(2,1)S(1)}, u32[]{:S(2)}, u32[]{:S(2)}) async-start(bf16[64,16,128]{2,1,0:T(8,128)(2,1)} %shard_map.82), calls=%async_computation.1 | async-start | bytes 524288 | tf_op jit(solution)/shard_map/all_to_all | solution.py:200
  101.0 3.5 %collective-permute-start.11 = (f32[512,128]{1,0:T(8,128)S(1)}, f32[512,128]{1,0:T(8,128)S(1)}, u32[]{:S(2)}, u32[]{:S(2)}) collective-permute-start(f32[512,128]{1,0:T(8,128)S(1)} %slice.115), channel_id=1, source_target_pairs={{0,1},{1,0},{2,3},{3,2},{4,5},{5,4},{6,7},{7,6},{8,9},{9,8},{10,11... | collective-permute-start | bytes 786440 | tf_op jit(solution)/shard_map/ppermute | solution.py:59
  104.5 9.9 %all-to-all-done.1 = bf16[64,16,128]{2,1,0:T(8,128)(2,1)S(1)} async-done(((bf16[64,16,128]{2,1,0:T(8,128)(2,1)}), bf16[64,16,128]{2,1,0:T(8,128)(2,1)S(1)}, u32[]{:S(2)}, u32[]{:S(2)}) %all-to-all-start.1) | async-done | bytes 262176 | tf_op jit(solution)/shard_map/all_to_all | solution.py:200
  116.3 2.0 %fusion.27 = bf16[64,8,128]{2,1,0:T(8,128)(2,1)} fusion(f32[512,128]{1,0:T(8,128)S(1)} %collective-permute-done.11, f32[512,256]{1,0:T(8,128)S(1)} %bitcast.138, bf16[512,4096]{0,1:T(8,128)(2,1)S(1)} %bitcast.133, bf16[4096,128]{1,0:T(8,128)(2,1)S(1)} %bitcast.142), kind=kOutput, calls=%fused_computation.58 | convolution fusion | flops 537133056 | bytes 5898240 | tf_op jit(solution)/shard_map/dot_general | solution.py:214
  118.2 5.7 %all-to-all-start.2 = ((bf16[64,8,128]{2,1,0:T(8,128)(2,1)}), bf16[64,8,128]{2,1,0:T(8,128)(2,1)S(1)}, u32[]{:S(2)}, u32[]{:S(2)}) async-start(bf16[64,8,128]{2,1,0:T(8,128)(2,1)} %fusion.27), calls=%async_computation.2 | async-start | bytes 262144 | tf_op jit(solution)/shard_map/all_to_all | solution.py:220
  124.9 11.7 %all-to-all-done.2 = bf16[64,8,128]{2,1,0:T(8,128)(2,1)S(1)} async-done(((bf16[64,8,128]{2,1,0:T(8,128)(2,1)}), bf16[64,8,128]{2,1,0:T(8,128)(2,1)S(1)}, u32[]{:S(2)}, u32[]{:S(2)}) %all-to-all-start.2) | async-done | bytes 131104 | tf_op jit(solution)/shard_map/all_to_all | solution.py:220
  (87 shorter events, 23.2 us)
Async XLA Ops:
  0.0 1.6 %copy-start = (bf16[1,8192,128]{2,1,0:T(8,128)(2,1)S(1)}, bf16[1,8192,128]{2,1,0:T(8,128)(2,1)}, u32[]{:S(2)}) copy-start(bf16[1,8192,128]{2,1,0:T(8,128)(2,1)} %param.10) | copy-start | bytes 6291460
  0.0 6.4 %copy-start.5 = (f32[1,8192]{1,0:T(1,128)S(1)}, f32[1,8192]{1,0:T(1,128)}, u32[]{:S(2)}) copy-start(f32[1,8192]{1,0:T(1,128)} %param.9) | copy-start | bytes 98308
  0.0 6.3 %collective-permute-start = (bf16[8,8192]{1,0:T(8,128)(2,1)}, bf16[8,8192]{1,0:T(8,128)(2,1)S(1)}, u32[]{:S(2)}, u32[]{:S(2)}) collective-permute-start(bf16[8,8192]{1,0:T(8,128)(2,1)} %param.8), channel_id=1, source_target_pairs={{0,64},{64,128},{128,192},{192,256},{256,320},{320,384},{384,448},... | collective-permute-start | bytes 393224 | tf_op jit(solution)/shard_map/ppermute | solution.py:37
  1.6 12.0 %copy-start.4 = (s32[512]{0:T(512)S(1)}, s32[512]{0:T(512)}, u32[]{:S(2)}) copy-start(s32[512]{0:T(512)} %param.13) | copy-start | bytes 6148
  2.6 39.2 %collective-permute-start.10 = (bf16[4096,128]{1,0:T(8,128)(2,1)}, bf16[4096,128]{1,0:T(8,128)(2,1)}, u32[]{:S(2)}, u32[]{:S(2)}) collective-permute-start(bf16[4096,128]{1,0:T(8,128)(2,1)} %dynamic-slice_bitcast_fusion), channel_id=1, source_target_pairs={{0,1},{1,0},{2,3},{3,2},{4,5},{5,4},{6,7},{7,6},{8,9},{9,8},{10,11... | collective-permute-start | bytes 3145736 | tf_op jit(solution)/shard_map/ppermute | solution.py:59
  7.4 21.5 %all-to-all-start = ((bf16[8,8,4096]{2,1,0:T(8,128)(2,1)}), bf16[8,8,4096]{2,1,0:T(8,128)(2,1)S(1)}, u32[]{:S(2)}, u32[]{:S(2)}) async-start(bf16[8,8,4096]{2,1,0:T(8,128)(2,1)} %bitcast.12), calls=%async_computation | async-start | bytes 1048576 | tf_op jit(solution)/shard_map/all_to_all | solution.py:47
  28.9 17.6 %collective-permute-start.2 = (bf16[64,4096]{1,0:T(8,128)(2,1)S(1)}, bf16[64,4096]{1,0:T(8,128)(2,1)S(1)}, u32[]{:S(2)}, u32[]{:S(2)}) collective-permute-start(bf16[64,4096]{1,0:T(8,128)(2,1)S(1)} %bitcast.134), channel_id=1, source_target_pairs={{0,56},{8,0},{16,8},{24,16},{32,24},{40,32},{48,40},{56,48},{1,57}... | collective-permute-start | bytes 1572872 | tf_op jit(solution)/shard_map/ppermute | solution.py:54
  39.9 12.3 %collective-permute-start.1 = (bf16[64,4096]{1,0:T(8,128)(2,1)S(1)}, bf16[64,4096]{1,0:T(8,128)(2,1)S(1)}, u32[]{:S(2)}, u32[]{:S(2)}) collective-permute-start(bf16[64,4096]{1,0:T(8,128)(2,1)S(1)} %bitcast.135), channel_id=1, source_target_pairs={{0,8},{8,16},{16,24},{24,32},{32,40},{40,48},{48,56},{56,0},{1,9},... | collective-permute-start | bytes 1572872 | tf_op jit(solution)/shard_map/ppermute | solution.py:54
  46.5 12.3 %collective-permute-start.4 = (bf16[64,4096]{1,0:T(8,128)(2,1)S(1)}, bf16[64,4096]{1,0:T(8,128)(2,1)S(1)}, u32[]{:S(2)}, u32[]{:S(2)}) collective-permute-start(bf16[64,4096]{1,0:T(8,128)(2,1)S(1)} %collective-permute-done.2), channel_id=1, source_target_pairs={{0,56},{8,0},{16,8},{24,16},{32,24},{40,32},{48,40},{56,48},{1,57}... | collective-permute-start | bytes 1572872 | tf_op jit(solution)/shard_map/ppermute | solution.py:54
  52.2 12.3 %collective-permute-start.3 = (bf16[64,4096]{1,0:T(8,128)(2,1)S(1)}, bf16[64,4096]{1,0:T(8,128)(2,1)S(1)}, u32[]{:S(2)}, u32[]{:S(2)}) collective-permute-start(bf16[64,4096]{1,0:T(8,128)(2,1)S(1)} %collective-permute-done.1), channel_id=1, source_target_pairs={{0,8},{8,16},{16,24},{24,32},{32,40},{40,48},{48,56},{56,0},{1,9},... | collective-permute-start | bytes 1572872 | tf_op jit(solution)/shard_map/ppermute | solution.py:54
  58.8 16.6 %collective-permute-start.8 = (bf16[64,2048]{1,0:T(8,128)(2,1)S(1)}, bf16[64,2048]{1,0:T(8,128)(2,1)S(1)}, u32[]{:S(2)}, u32[]{:S(2)}) collective-permute-start(bf16[64,2048]{1,0:T(8,128)(2,1)S(1)} %slice.109), channel_id=1, source_target_pairs={{0,48},{8,56},{16,0},{24,8},{32,16},{40,24},{48,32},{56,40},{1,49}... | collective-permute-start | bytes 786440 | tf_op jit(solution)/shard_map/ppermute | solution.py:54
  64.5 12.6 %collective-permute-start.7 = (bf16[64,2048]{1,0:T(8,128)(2,1)S(1)}, bf16[64,2048]{1,0:T(8,128)(2,1)S(1)}, u32[]{:S(2)}, u32[]{:S(2)}) collective-permute-start(bf16[64,2048]{1,0:T(8,128)(2,1)S(1)} %slice.108), channel_id=1, source_target_pairs={{0,16},{8,24},{16,32},{24,40},{32,48},{40,56},{48,0},{56,8},{1,17}... | collective-permute-start | bytes 786440 | tf_op jit(solution)/shard_map/ppermute | solution.py:54
  66.4 12.7 %collective-permute-start.6 = (bf16[64,4096]{1,0:T(8,128)(2,1)S(1)}, bf16[64,4096]{1,0:T(8,128)(2,1)S(1)}, u32[]{:S(2)}, u32[]{:S(2)}) collective-permute-start(bf16[64,4096]{1,0:T(8,128)(2,1)S(1)} %collective-permute-done.4), channel_id=1, source_target_pairs={{0,56},{8,0},{16,8},{24,16},{32,24},{40,32},{48,40},{56,48},{1,57}... | collective-permute-start | bytes 1572872 | tf_op jit(solution)/shard_map/ppermute | solution.py:54
  72.5 12.3 %collective-permute-start.5 = (bf16[64,4096]{1,0:T(8,128)(2,1)S(1)}, bf16[64,4096]{1,0:T(8,128)(2,1)S(1)}, u32[]{:S(2)}, u32[]{:S(2)}) collective-permute-start(bf16[64,4096]{1,0:T(8,128)(2,1)S(1)} %collective-permute-done.3), channel_id=1, source_target_pairs={{0,8},{8,16},{16,24},{24,32},{32,40},{40,48},{48,56},{56,0},{1,9},... | collective-permute-start | bytes 1572872 | tf_op jit(solution)/shard_map/ppermute | solution.py:54
  85.2 8.3 %collective-permute-start.9 = (bf16[32,4096]{1,0:T(8,128)(2,1)S(1)}, bf16[32,4096]{1,0:T(8,128)(2,1)S(1)}, u32[]{:S(2)}, u32[]{:S(2)}) collective-permute-start(bf16[32,4096]{1,0:T(8,128)(2,1)S(1)} %get-tuple-element.13), channel_id=1, source_target_pairs={{0,1},{1,0},{2,3},{3,2},{4,5},{5,4},{6,7},{7,6},{8,9},{9,8},{10,11... | collective-permute-start | bytes 786440 | tf_op jit(solution)/shard_map/ppermute | solution.py:59
  89.1 4.4 %copy-start.1 = (bf16[1,1,8192,64]{2,3,1,0:T(8,128)(2,1)S(1)}, bf16[1,1,8192,64]{2,3,1,0:T(8,128)(2,1)}, u32[]{:S(2)}) copy-start(bf16[1,1,8192,64]{2,3,1,0:T(8,128)(2,1)} %param.11) | copy-start | bytes 3145732
  94.6 19.7 %all-to-all-start.1 = ((bf16[64,16,128]{2,1,0:T(8,128)(2,1)}), bf16[64,16,128]{2,1,0:T(8,128)(2,1)S(1)}, u32[]{:S(2)}, u32[]{:S(2)}) async-start(bf16[64,16,128]{2,1,0:T(8,128)(2,1)} %shard_map.82), calls=%async_computation.1 | async-start | bytes 524288 | tf_op jit(solution)/shard_map/all_to_all | solution.py:200
  101.0 14.4 %collective-permute-start.11 = (f32[512,128]{1,0:T(8,128)S(1)}, f32[512,128]{1,0:T(8,128)S(1)}, u32[]{:S(2)}, u32[]{:S(2)}) collective-permute-start(f32[512,128]{1,0:T(8,128)S(1)} %slice.115), channel_id=1, source_target_pairs={{0,1},{1,0},{2,3},{3,2},{4,5},{5,4},{6,7},{7,6},{8,9},{9,8},{10,11... | collective-permute-start | bytes 786440 | tf_op jit(solution)/shard_map/ppermute | solution.py:59
  115.0 1.2 copy-start.2
  116.3 7.6 %copy-start.3 = (bf16[8,2,16,1024]{3,2,1,0:T(8,128)(2,1)S(1)}, bf16[8,2,16,1024]{3,2,1,0:T(8,128)(2,1)}, u32[]{:S(2)}) copy-start(bf16[8,2,16,1024]{3,2,1,0:T(8,128)(2,1)} %param.15) | copy-start | bytes 1572868
  118.2 18.4 %all-to-all-start.2 = ((bf16[64,8,128]{2,1,0:T(8,128)(2,1)}), bf16[64,8,128]{2,1,0:T(8,128)(2,1)S(1)}, u32[]{:S(2)}, u32[]{:S(2)}) async-start(bf16[64,8,128]{2,1,0:T(8,128)(2,1)} %fusion.27), calls=%async_computation.2 | async-start | bytes 262144 | tf_op jit(solution)/shard_map/all_to_all | solution.py:220

commit v4 on v3

--- a/solution.py
+++ b/solution.py
@@ -222,21 +222,24 @@
     )
     own_lengths = lax.dynamic_slice_in_dim(cache_valid_length, position * tok_dev, tok_dev)
     group_size = HEADS // KVH
-    query_heads = own_queries.reshape(KVH, group_size, tok_dev, HD)
-    cached_keys = key_value_cache[:, 0].reshape(tok_dev, CTX, KVH, HD)
-    cached_values = key_value_cache[:, 1].reshape(tok_dev, CTX, KVH, HD)
+    queries = own_queries.reshape(KVH, group_size * tok_dev, HD)
+    cache = key_value_cache.reshape(tok_dev, 2, CTX, KVH, HD).transpose(1, 3, 0, 2, 4)
+    cached_keys = cache[0].reshape(KVH, tok_dev * CTX, HD)
+    cached_values = cache[1].reshape(KVH, tok_dev * CTX, HD)
+    row_token = jnp.arange(group_size * tok_dev, dtype=jnp.int32)[:, None] % tok_dev
+    column = jnp.arange(tok_dev * CTX, dtype=jnp.int32)[None, :]
+    live = jnp.tile(own_lengths, group_size)[:, None]
+    seen = (column // CTX == row_token) & (column % CTX < live)
     scores = jnp.einsum(
-        "kgtd,tckd->tkgc", query_heads, cached_keys, preferred_element_type=jnp.float32
+        "krd,kcd->krc", queries, cached_keys, preferred_element_type=jnp.float32
     ) * HD ** (-0.5)
-    is_live = jnp.arange(CTX, dtype=jnp.int32)[None, :] < own_lengths[:, None]
-    scores = jnp.where(is_live[:, None, None, :], scores, -jnp.inf)
+    scores = jnp.where(seen[None], scores, -jnp.inf)
     row_max = jnp.max(scores, axis=-1, keepdims=True)
     expsum = jnp.exp(scores - row_max)
     probs = (expsum / jnp.sum(expsum, axis=-1, keepdims=True)).astype(jnp.bfloat16)
-    context = jnp.einsum(
-        "tkgc,tckd->tkgd", probs, cached_values, preferred_element_type=jnp.float32
-    )
-    return context.astype(jnp.bfloat16).reshape(tok_dev, MODEL_WIDTH)
+    context = jnp.einsum("krc,kcd->krd", probs, cached_values, preferred_element_type=jnp.float32)
+    context = context.astype(jnp.bfloat16).reshape(HEADS, tok_dev, HD)
+    return context.transpose(1, 0, 2).reshape(tok_dev, MODEL_WIDTH)
 
 
 def solution(mesh):

time: 140 us -> 143 us (1.021)
  the two profiles are of different devices: /device:TPU:2 before, /device:TPU:8 now
where the time goes in v4:
time: 143 us; the launch traced here: 142 us
  starting transfers between devices  62.9 us (44%)
  waiting for transfers between devices  53.9 us (38%)
  matrix products  11.8 us (8%)
  local copies, waits for them, and re-layouts  7.53 us (5%)
  other arithmetic  4.42 us (3%)
    ppermute x8, starting transfers between devices, along_line(): return lax.ppermute(block, BOTH, pairs)  33.3 us
    ppermute x8, waiting for transfers between devices, along_line(): return lax.ppermute(block, BOTH, pairs)  15.9 us
    ppermute x3, starting transfers between devices, to_partner(): return lax.ppermute(block, BOTH, pairs)  13.3 us
    all_to_all x1, waiting for transfers between devices, body(): lax.all_to_all(query_rows.reshape(HEADS, tok_dev, HD), 'adapter', split_a...  11.6 us
    all_to_all x1, waiting for transfers between devices, body(): lax.all_to_all(shrunk, 'adapter', split_axis=0, concat_axis=0, tiled=True)  10.3 us
    all_to_all x1, waiting for transfers between devices, over_line(): lax.all_to_all(blocks, BOTH, split_axis=0, concat_axis=0, tiled=True, axi...  8.13 us
    all_to_all x1, starting transfers between devices, body(): lax.all_to_all(shrunk, 'adapter', split_axis=0, concat_axis=0, tiled=True)  7.54 us
    all_to_all x1, starting transfers between devices, body(): lax.all_to_all(query_rows.reshape(HEADS, tok_dev, HD), 'adapter', split_a...  5.34 us
  transfers between devices with their start and end apart: 15, of which 11 were waited for; matrix products, arithmetic and copies ran while one was open for 11% of the time, Pallas kernels for 0%

profile of v4, /device:TPU:8, one launch (start us, length us, event | category | flops | bytes accessed | tf_op | source)
XLA Modules:
  0.0 142.4 jit_solution(15832450324310936711)
XLA Ops:
  2.6 7.7 %collective-permute-start.10 = (bf16[4096,128]{1,0:T(8,128)(2,1)}, bf16[4096,128]{1,0:T(8,128)(2,1)}, u32[]{:S(2)}, u32[]{:S(2)}) collective-permute-start(bf16[4096,128]{1,0:T(8,128)(2,1)} %dynamic-slice_bitcast_fusion), channel_id=1, source_target_pairs={{0,1},{1,0},{2,3},{3,2},{4,5},{5,4},{6,7},{7,6},{8,9},{9,8},{10,11... | collective-permute-start | bytes 3145736 | tf_op jit(solution)/shard_map/ppermute | solution.py:59
  11.3 4.6 %collective-permute-done = bf16[8,8192]{1,0:T(8,128)(2,1)S(1)} collective-permute-done((bf16[8,8192]{1,0:T(8,128)(2,1)S(1)}, bf16[8,8192]{1,0:T(8,128)(2,1)S(1)}, u32[]{:S(2)}, u32[]{:S(2)}) %collective-permute-start) | collective-permute-done | bytes 131104 | tf_op jit(solution)/shard_map/ppermute | solution.py:37
  17.1 3.4 %all-to-all-start = ((bf16[8,8,4096]{2,1,0:T(8,128)(2,1)}), bf16[8,8,4096]{2,1,0:T(8,128)(2,1)S(1)}, u32[]{:S(2)}, u32[]{:S(2)}) async-start(bf16[8,8,4096]{2,1,0:T(8,128)(2,1)} %bitcast.12), calls=%async_computation | async-start | bytes 1048576 | tf_op jit(solution)/shard_map/all_to_all | solution.py:47
  24.2 8.1 %all-to-all-done = bf16[8,8,4096]{2,1,0:T(8,128)(2,1)S(1)} async-done(((bf16[8,8,4096]{2,1,0:T(8,128)(2,1)}), bf16[8,8,4096]{2,1,0:T(8,128)(2,1)S(1)}, u32[]{:S(2)}, u32[]{:S(2)}) %all-to-all-start) | async-done | bytes 524320 | tf_op jit(solution)/shard_map/all_to_all | solution.py:47
  32.4 10.1 %collective-permute-start.2 = (bf16[64,4096]{1,0:T(8,128)(2,1)S(1)}, bf16[64,4096]{1,0:T(8,128)(2,1)S(1)}, u32[]{:S(2)}, u32[]{:S(2)}) collective-permute-start(bf16[64,4096]{1,0:T(8,128)(2,1)S(1)} %bitcast.134), channel_id=1, source_target_pairs={{0,56},{8,0},{16,8},{24,16},{32,24},{40,32},{48,40},{56,48},{1,57}... | collective-permute-start | bytes 1572872 | tf_op jit(solution)/shard_map/ppermute | solution.py:54
  42.5 1.9 %collective-permute-start.1 = (bf16[64,4096]{1,0:T(8,128)(2,1)S(1)}, bf16[64,4096]{1,0:T(8,128)(2,1)S(1)}, u32[]{:S(2)}, u32[]{:S(2)}) collective-permute-start(bf16[64,4096]{1,0:T(8,128)(2,1)S(1)} %bitcast.135), channel_id=1, source_target_pairs={{0,8},{8,16},{16,24},{24,32},{32,40},{40,48},{48,56},{56,0},{1,9},... | collective-permute-start | bytes 1572872 | tf_op jit(solution)/shard_map/ppermute | solution.py:54
  44.4 1.8 %pad_maximum_fusion = bf16[4096,256]{1,0:T(8,128)(2,1)S(1)} fusion(bf16[4096,128]{1,0:T(8,128)(2,1)} %collective-permute-done.10, bf16[4096,128]{1,0:T(8,128)(2,1)} %constant_dynamic-slice_fusion), kind=kLoop, calls=%fused_computation.17 | loop fusion | flops 4194304 | bytes 4194304 | tf_op jit(solution)/shard_map/concatenate | solution.py:141
  47.0 2.2 %collective-permute-done.2 = bf16[64,4096]{1,0:T(8,128)(2,1)S(1)} collective-permute-done((bf16[64,4096]{1,0:T(8,128)(2,1)S(1)}, bf16[64,4096]{1,0:T(8,128)(2,1)S(1)}, u32[]{:S(2)}, u32[]{:S(2)}) %collective-permute-start.2) | collective-permute-done | bytes 524320 | tf_op jit(solution)/shard_map/ppermute | solution.py:54
  49.2 5.6 %collective-permute-start.4 = (bf16[64,4096]{1,0:T(8,128)(2,1)S(1)}, bf16[64,4096]{1,0:T(8,128)(2,1)S(1)}, u32[]{:S(2)}, u32[]{:S(2)}) collective-permute-start(bf16[64,4096]{1,0:T(8,128)(2,1)S(1)} %collective-permute-done.2), channel_id=1, source_target_pairs={{0,56},{8,0},{16,8},{24,16},{32,24},{40,32},{48,40},{56,48},{1,57}... | collective-permute-start | bytes 1572872 | tf_op jit(solution)/shard_map/ppermute | solution.py:54
  54.8 1.9 %collective-permute-start.3 = (bf16[64,4096]{1,0:T(8,128)(2,1)S(1)}, bf16[64,4096]{1,0:T(8,128)(2,1)S(1)}, u32[]{:S(2)}, u32[]{:S(2)}) collective-permute-start(bf16[64,4096]{1,0:T(8,128)(2,1)S(1)} %collective-permute-done.1), channel_id=1, source_target_pairs={{0,8},{8,16},{16,24},{24,32},{32,40},{40,48},{48,56},{56,0},{1,9},... | collective-permute-start | bytes 1572872 | tf_op jit(solution)/shard_map/ppermute | solution.py:54
  57.8 3.7 %collective-permute-done.4 = bf16[64,4096]{1,0:T(8,128)(2,1)S(1)} collective-permute-done((bf16[64,4096]{1,0:T(8,128)(2,1)S(1)}, bf16[64,4096]{1,0:T(8,128)(2,1)S(1)}, u32[]{:S(2)}, u32[]{:S(2)}) %collective-permute-start.4) | collective-permute-done | bytes 524320 | tf_op jit(solution)/shard_map/ppermute | solution.py:54
  61.5 3.8 %collective-permute-start.8 = (bf16[64,2048]{1,0:T(8,128)(2,1)S(1)}, bf16[64,2048]{1,0:T(8,128)(2,1)S(1)}, u32[]{:S(2)}, u32[]{:S(2)}) collective-permute-start(bf16[64,2048]{1,0:T(8,128)(2,1)S(1)} %slice.109), channel_id=1, source_target_pairs={{0,48},{8,56},{16,0},{24,8},{32,16},{40,24},{48,32},{56,40},{1,49}... | collective-permute-start | bytes 786440 | tf_op jit(solution)/shard_map/ppermute | solution.py:54
  67.1 1.9 %collective-permute-start.7 = (bf16[64,2048]{1,0:T(8,128)(2,1)S(1)}, bf16[64,2048]{1,0:T(8,128)(2,1)S(1)}, u32[]{:S(2)}, u32[]{:S(2)}) collective-permute-start(bf16[64,2048]{1,0:T(8,128)(2,1)S(1)} %slice.108), channel_id=1, source_target_pairs={{0,16},{8,24},{16,32},{24,40},{32,48},{40,56},{48,0},{56,8},{1,17}... | collective-permute-start | bytes 786440 | tf_op jit(solution)/shard_map/ppermute | solution.py:54
  69.0 6.1 %collective-permute-start.6 = (bf16[64,4096]{1,0:T(8,128)(2,1)S(1)}, bf16[64,4096]{1,0:T(8,128)(2,1)S(1)}, u32[]{:S(2)}, u32[]{:S(2)}) collective-permute-start(bf16[64,4096]{1,0:T(8,128)(2,1)S(1)} %collective-permute-done.4), channel_id=1, source_target_pairs={{0,56},{8,0},{16,8},{24,16},{32,24},{40,32},{48,40},{56,48},{1,57}... | collective-permute-start | bytes 1572872 | tf_op jit(solution)/shard_map/ppermute | solution.py:54
  75.1 1.9 %collective-permute-start.5 = (bf16[64,4096]{1,0:T(8,128)(2,1)S(1)}, bf16[64,4096]{1,0:T(8,128)(2,1)S(1)}, u32[]{:S(2)}, u32[]{:S(2)}) collective-permute-start(bf16[64,4096]{1,0:T(8,128)(2,1)S(1)} %collective-permute-done.3), channel_id=1, source_target_pairs={{0,8},{8,16},{16,24},{24,32},{32,40},{40,48},{48,56},{56,0},{1,9},... | collective-permute-start | bytes 1572872 | tf_op jit(solution)/shard_map/ppermute | solution.py:54
  82.0 5.3 %collective-permute-done.5 = bf16[64,4096]{1,0:T(8,128)(2,1)S(1)} collective-permute-done((bf16[64,4096]{1,0:T(8,128)(2,1)S(1)}, bf16[64,4096]{1,0:T(8,128)(2,1)S(1)}, u32[]{:S(2)}, u32[]{:S(2)}) %collective-permute-start.5) | collective-permute-done | bytes 524320 | tf_op jit(solution)/shard_map/ppermute | solution.py:54
  87.8 3.2 %collective-permute-start.9 = (bf16[32,4096]{1,0:T(8,128)(2,1)S(1)}, bf16[32,4096]{1,0:T(8,128)(2,1)S(1)}, u32[]{:S(2)}, u32[]{:S(2)}) collective-permute-start(bf16[32,4096]{1,0:T(8,128)(2,1)S(1)} %get-tuple-element.15), channel_id=1, source_target_pairs={{0,1},{1,0},{2,3},{3,2},{4,5},{5,4},{6,7},{7,6},{8,9},{9,8},{10,11... | collective-permute-start | bytes 786440 | tf_op jit(solution)/shard_map/ppermute | solution.py:59
  93.2 3.3 %collective-permute-done.9.theirs_ref = bf16[32,4096]{1,0:T(8,128)(2,1)S(1)} collective-permute-done((bf16[32,4096]{1,0:T(8,128)(2,1)S(1)}, bf16[32,4096]{1,0:T(8,128)(2,1)S(1)}, u32[]{:S(2)}, u32[]{:S(2)}) %collective-permute-start.9) | collective-permute-done | bytes 262176 | tf_op jit(solution)/shard_map/ppermute | solution.py:59
  97.7 7.5 %all-to-all-start.1 = ((bf16[64,16,128]{2,1,0:T(8,128)(2,1)}), bf16[64,16,128]{2,1,0:T(8,128)(2,1)}, u32[]{:S(2)}, u32[]{:S(2)}) async-start(bf16[64,16,128]{2,1,0:T(8,128)(2,1)} %shard_map.82), calls=%async_computation.1 | async-start | bytes 524288 | tf_op jit(solution)/shard_map/all_to_all | solution.py:200
  105.4 2.4 %collective-permute-start.11 = (f32[512,128]{1,0:T(8,128)S(1)}, f32[512,128]{1,0:T(8,128)S(1)}, u32[]{:S(2)}, u32[]{:S(2)}) collective-permute-start(f32[512,128]{1,0:T(8,128)S(1)} %slice.115), channel_id=1, source_target_pairs={{0,1},{1,0},{2,3},{3,2},{4,5},{5,4},{6,7},{7,6},{8,9},{9,8},{10,11... | collective-permute-start | bytes 786440 | tf_op jit(solution)/shard_map/ppermute | solution.py:59
  107.9 10.3 %all-to-all-done.1 = bf16[64,16,128]{2,1,0:T(8,128)(2,1)} async-done(((bf16[64,16,128]{2,1,0:T(8,128)(2,1)}), bf16[64,16,128]{2,1,0:T(8,128)(2,1)}, u32[]{:S(2)}, u32[]{:S(2)}) %all-to-all-start.1) | async-done | bytes 262176 | tf_op jit(solution)/shard_map/all_to_all | solution.py:200
  121.1 2.0 %fusion.24 = bf16[64,8,128]{2,1,0:T(8,128)(2,1)} fusion(f32[512,128]{1,0:T(8,128)S(1)} %collective-permute-done.11, f32[512,256]{1,0:T(8,128)S(1)} %bitcast.138, bf16[512,4096]{0,1:T(8,128)(2,1)S(1)} %bitcast.133, bf16[4096,128]{1,0:T(8,128)(2,1)S(1)} %bitcast.141), kind=kOutput, calls=%fused_computation.56 | convolution fusion | flops 537133056 | bytes 5898240 | tf_op jit(solution)/shard_map/dot_general | solution.py:214
  123.0 5.3 %all-to-all-start.2 = ((bf16[64,8,128]{2,1,0:T(8,128)(2,1)}), bf16[64,8,128]{2,1,0:T(8,128)(2,1)S(1)}, u32[]{:S(2)}, u32[]{:S(2)}) async-start(bf16[64,8,128]{2,1,0:T(8,128)(2,1)} %fusion.24), calls=%async_computation.2 | async-start | bytes 262144 | tf_op jit(solution)/shard_map/all_to_all | solution.py:220
  128.7 11.6 %all-to-all-done.2 = bf16[64,8,128]{2,1,0:T(8,128)(2,1)S(1)} async-done(((bf16[64,8,128]{2,1,0:T(8,128)(2,1)}), bf16[64,8,128]{2,1,0:T(8,128)(2,1)S(1)}, u32[]{:S(2)}, u32[]{:S(2)}) %all-to-all-start.2) | async-done | bytes 131104 | tf_op jit(solution)/shard_map/all_to_all | solution.py:220
  (92 shorter events, 26.0 us)
Async XLA Ops:
  0.0 1.6 %copy-start = (bf16[1,8192,128]{2,1,0:T(8,128)(2,1)S(1)}, bf16[1,8192,128]{2,1,0:T(8,128)(2,1)}, u32[]{:S(2)}) copy-start(bf16[1,8192,128]{2,1,0:T(8,128)(2,1)} %param.10) | copy-start | bytes 6291460
  0.0 10.4 %copy-start.6 = (bf16[8,8192]{1,0:T(8,128)(2,1)S(1)}, bf16[8,8192]{1,0:T(8,128)(2,1)}, u32[]{:S(2)}) copy-start(bf16[8,8192]{1,0:T(8,128)(2,1)} %param.8) | copy-start | bytes 393220
  0.0 16.2 %copy-start.5 = (f32[1,8192]{1,0:T(1,128)S(1)}, f32[1,8192]{1,0:T(1,128)}, u32[]{:S(2)}) copy-start(f32[1,8192]{1,0:T(1,128)} %param.9) | copy-start | bytes 98308
  1.6 19.0 %copy-start.4 = (s32[512]{0:T(512)S(1)}, s32[512]{0:T(512)}, u32[]{:S(2)}) copy-start(s32[512]{0:T(512)} %param.13) | copy-start | bytes 6148
  2.6 41.8 %collective-permute-start.10 = (bf16[4096,128]{1,0:T(8,128)(2,1)}, bf16[4096,128]{1,0:T(8,128)(2,1)}, u32[]{:S(2)}, u32[]{:S(2)}) collective-permute-start(bf16[4096,128]{1,0:T(8,128)(2,1)} %dynamic-slice_bitcast_fusion), channel_id=1, source_target_pairs={{0,1},{1,0},{2,3},{3,2},{4,5},{5,4},{6,7},{7,6},{8,9},{9,8},{10,11... | collective-permute-start | bytes 3145736 | tf_op jit(solution)/shard_map/ppermute | solution.py:59
  10.4 5.6 %collective-permute-start = (bf16[8,8192]{1,0:T(8,128)(2,1)S(1)}, bf16[8,8192]{1,0:T(8,128)(2,1)S(1)}, u32[]{:S(2)}, u32[]{:S(2)}) collective-permute-start(bf16[8,8192]{1,0:T(8,128)(2,1)S(1)} %copy-done.6), channel_id=1, source_target_pairs={{0,64},{64,128},{128,192},{192,256},{256,320},{320,384},{384,448},... | collective-permute-start | bytes 393224 | tf_op jit(solution)/shard_map/ppermute | solution.py:37
  17.1 15.3 %all-to-all-start = ((bf16[8,8,4096]{2,1,0:T(8,128)(2,1)}), bf16[8,8,4096]{2,1,0:T(8,128)(2,1)S(1)}, u32[]{:S(2)}, u32[]{:S(2)}) async-start(bf16[8,8,4096]{2,1,0:T(8,128)(2,1)} %bitcast.12), calls=%async_computation | async-start | bytes 1048576 | tf_op jit(solution)/shard_map/all_to_all | solution.py:47
  32.4 16.8 %collective-permute-start.2 = (bf16[64,4096]{1,0:T(8,128)(2,1)S(1)}, bf16[64,4096]{1,0:T(8,128)(2,1)S(1)}, u32[]{:S(2)}, u32[]{:S(2)}) collective-permute-start(bf16[64,4096]{1,0:T(8,128)(2,1)S(1)} %bitcast.134), channel_id=1, source_target_pairs={{0,56},{8,0},{16,8},{24,16},{32,24},{40,32},{48,40},{56,48},{1,57}... | collective-permute-start | bytes 1572872 | tf_op jit(solution)/shard_map/ppermute | solution.py:54
  42.5 12.3 %collective-permute-start.1 = (bf16[64,4096]{1,0:T(8,128)(2,1)S(1)}, bf16[64,4096]{1,0:T(8,128)(2,1)S(1)}, u32[]{:S(2)}, u32[]{:S(2)}) collective-permute-start(bf16[64,4096]{1,0:T(8,128)(2,1)S(1)} %bitcast.135), channel_id=1, source_target_pairs={{0,8},{8,16},{16,24},{24,32},{32,40},{40,48},{48,56},{56,0},{1,9},... | collective-permute-start | bytes 1572872 | tf_op jit(solution)/shard_map/ppermute | solution.py:54
  49.2 12.3 %collective-permute-start.4 = (bf16[64,4096]{1,0:T(8,128)(2,1)S(1)}, bf16[64,4096]{1,0:T(8,128)(2,1)S(1)}, u32[]{:S(2)}, u32[]{:S(2)}) collective-permute-start(bf16[64,4096]{1,0:T(8,128)(2,1)S(1)} %collective-permute-done.2), channel_id=1, source_target_pairs={{0,56},{8,0},{16,8},{24,16},{32,24},{40,32},{48,40},{56,48},{1,57}... | collective-permute-start | bytes 1572872 | tf_op jit(solution)/shard_map/ppermute | solution.py:54
  54.8 12.3 %collective-permute-start.3 = (bf16[64,4096]{1,0:T(8,128)(2,1)S(1)}, bf16[64,4096]{1,0:T(8,128)(2,1)S(1)}, u32[]{:S(2)}, u32[]{:S(2)}) collective-permute-start(bf16[64,4096]{1,0:T(8,128)(2,1)S(1)} %collective-permute-done.1), channel_id=1, source_target_pairs={{0,8},{8,16},{16,24},{24,32},{32,40},{40,48},{48,56},{56,0},{1,9},... | collective-permute-start | bytes 1572872 | tf_op jit(solution)/shard_map/ppermute | solution.py:54
  61.5 16.6 %collective-permute-start.8 = (bf16[64,2048]{1,0:T(8,128)(2,1)S(1)}, bf16[64,2048]{1,0:T(8,128)(2,1)S(1)}, u32[]{:S(2)}, u32[]{:S(2)}) collective-permute-start(bf16[64,2048]{1,0:T(8,128)(2,1)S(1)} %slice.109), channel_id=1, source_target_pairs={{0,48},{8,56},{16,0},{24,8},{32,16},{40,24},{48,32},{56,40},{1,49}... | collective-permute-start | bytes 786440 | tf_op jit(solution)/shard_map/ppermute | solution.py:54
  67.1 12.6 %collective-permute-start.7 = (bf16[64,2048]{1,0:T(8,128)(2,1)S(1)}, bf16[64,2048]{1,0:T(8,128)(2,1)S(1)}, u32[]{:S(2)}, u32[]{:S(2)}) collective-permute-start(bf16[64,2048]{1,0:T(8,128)(2,1)S(1)} %slice.108), channel_id=1, source_target_pairs={{0,16},{8,24},{16,32},{24,40},{32,48},{40,56},{48,0},{56,8},{1,17}... | collective-permute-start | bytes 786440 | tf_op jit(solution)/shard_map/ppermute | solution.py:54
  69.0 12.7 %collective-permute-start.6 = (bf16[64,4096]{1,0:T(8,128)(2,1)S(1)}, bf16[64,4096]{1,0:T(8,128)(2,1)S(1)}, u32[]{:S(2)}, u32[]{:S(2)}) collective-permute-start(bf16[64,4096]{1,0:T(8,128)(2,1)S(1)} %collective-permute-done.4), channel_id=1, source_target_pairs={{0,56},{8,0},{16,8},{24,16},{32,24},{40,32},{48,40},{56,48},{1,57}... | collective-permute-start | bytes 1572872 | tf_op jit(solution)/shard_map/ppermute | solution.py:54
  75.1 12.3 %collective-permute-start.5 = (bf16[64,4096]{1,0:T(8,128)(2,1)S(1)}, bf16[64,4096]{1,0:T(8,128)(2,1)S(1)}, u32[]{:S(2)}, u32[]{:S(2)}) collective-permute-start(bf16[64,4096]{1,0:T(8,128)(2,1)S(1)} %collective-permute-done.3), channel_id=1, source_target_pairs={{0,8},{8,16},{16,24},{24,32},{32,40},{40,48},{48,56},{56,0},{1,9},... | collective-permute-start | bytes 1572872 | tf_op jit(solution)/shard_map/ppermute | solution.py:54
  87.8 8.7 %collective-permute-start.9 = (bf16[32,4096]{1,0:T(8,128)(2,1)S(1)}, bf16[32,4096]{1,0:T(8,128)(2,1)S(1)}, u32[]{:S(2)}, u32[]{:S(2)}) collective-permute-start(bf16[32,4096]{1,0:T(8,128)(2,1)S(1)} %get-tuple-element.15), channel_id=1, source_target_pairs={{0,1},{1,0},{2,3},{3,2},{4,5},{5,4},{6,7},{7,6},{8,9},{9,8},{10,11... | collective-permute-start | bytes 786440 | tf_op jit(solution)/shard_map/ppermute | solution.py:59
  92.2 4.2 %copy-start.1 = (bf16[1,1,8192,64]{2,3,1,0:T(8,128)(2,1)S(1)}, bf16[1,1,8192,64]{2,3,1,0:T(8,128)(2,1)}, u32[]{:S(2)}) copy-start(bf16[1,1,8192,64]{2,3,1,0:T(8,128)(2,1)} %param.11) | copy-start | bytes 3145732
  97.7 20.5 %all-to-all-start.1 = ((bf16[64,16,128]{2,1,0:T(8,128)(2,1)}), bf16[64,16,128]{2,1,0:T(8,128)(2,1)}, u32[]{:S(2)}, u32[]{:S(2)}) async-start(bf16[64,16,128]{2,1,0:T(8,128)(2,1)} %shard_map.82), calls=%async_computation.1 | async-start | bytes 524288 | tf_op jit(solution)/shard_map/all_to_all | solution.py:200
  105.4 14.7 %collective-permute-start.11 = (f32[512,128]{1,0:T(8,128)S(1)}, f32[512,128]{1,0:T(8,128)S(1)}, u32[]{:S(2)}, u32[]{:S(2)}) collective-permute-start(f32[512,128]{1,0:T(8,128)S(1)} %slice.115), channel_id=1, source_target_pairs={{0,1},{1,0},{2,3},{3,2},{4,5},{5,4},{6,7},{7,6},{8,9},{9,8},{10,11... | collective-permute-start | bytes 786440 | tf_op jit(solution)/shard_map/ppermute | solution.py:59
  119.8 1.2 copy-start.2
  121.1 7.4 %copy-start.3 = (bf16[8,2,16,1024]{3,2,1,0:T(8,128)(2,1)S(1)}, bf16[8,2,16,1024]{3,2,1,0:T(8,128)(2,1)}, u32[]{:S(2)}) copy-start(bf16[8,2,16,1024]{3,2,1,0:T(8,128)(2,1)} %param.15) | copy-start | bytes 1572868
  123.0 17.3 %all-to-all-start.2 = ((bf16[64,8,128]{2,1,0:T(8,128)(2,1)}), bf16[64,8,128]{2,1,0:T(8,128)(2,1)S(1)}, u32[]{:S(2)}, u32[]{:S(2)}) async-start(bf16[64,8,128]{2,1,0:T(8,128)(2,1)} %fusion.24), calls=%async_computation.2 | async-start | bytes 262144 | tf_op jit(solution)/shard_map/all_to_all | solution.py:220

commit v5 on v3

--- a/solution.py
+++ b/solution.py
@@ -195,8 +195,11 @@
     products[far] = times(far_low, 0, quarter) + times(far_high, quarter, half)
     product = jnp.concatenate(products, axis=0)
     shrunk, product = lax.optimization_barrier((shrunk, product))
-    product = jnp.roll(product.reshape(SIDE, line_rows, -1), at_a, axis=0)
-    product = swap_sides(odd, product.reshape(segment_rows, -1))
+
+    def in_order(part):
+        part = jnp.roll(part.reshape(SIDE, line_rows, column_list), at_a, axis=0)
+        return swap_sides(odd, part.reshape(segment_rows, column_list))
+
     slots = lax.all_to_all(
         shrunk,
         "adapter",
@@ -205,7 +208,9 @@
         tiled=True,
     ).reshape(bank * some, 2 * rank_width)
 
-    base_query = product[:, :column_list] + to_partner(product[:, column_list:], lines_b)
+    base_query = in_order(product[:, :column_list]) + to_partner(
+        in_order(product[:, column_list:]), lines_b
+    )
     both = jnp.dot(place, slots, preferred_element_type=jnp.float32).astype(jnp.bfloat16)
     shrunk_tok = jnp.where(lower, both[:, :rank_width], both[:, rank_width:])
     spread = (named.astype(jnp.bfloat16)[:, :, None] * shrunk_tok[:, None, :]).reshape(

time: 140 us -> 139 us (level)
  no operation moved by 1% of the time
where the time goes in v5:
time: 139 us
  starting transfers between devices  61.6 us (44%)
  waiting for transfers between devices  52.5 us (38%)
  matrix products  10.2 us (7%)
  local copies, waits for them, and re-layouts  8.15 us (6%)
  other arithmetic  4.4 us (3%)
    ppermute x8, starting transfers between devices, along_line(): return lax.ppermute(block, BOTH, pairs)  34.1 us
    ppermute x8, waiting for transfers between devices, along_line(): return lax.ppermute(block, BOTH, pairs)  15.9 us
    all_to_all x1, waiting for transfers between devices, body(): lax.all_to_all(query_rows.reshape(HEADS, tok_dev, HD), 'adapter', split_a...  11.7 us
    all_to_all x1, waiting for transfers between devices, over_line(): lax.all_to_all(blocks, BOTH, split_axis=0, concat_axis=0, tiled=True, axi...  11.6 us
    all_to_all x1, waiting for transfers between devices, body(): lax.all_to_all(shrunk, 'adapter', split_axis=0, concat_axis=0, tiled=True)  9.91 us
    ppermute x3, starting transfers between devices, to_partner(): return lax.ppermute(block, BOTH, pairs)  9.57 us
    all_to_all x1, starting transfers between devices, over_line(): lax.all_to_all(blocks, BOTH, split_axis=0, concat_axis=0, tiled=True, axi...  6.2 us
    all_to_all x1, starting transfers between devices, body(): lax.all_to_all(shrunk, 'adapter', split_axis=0, concat_axis=0, tiled=True)  6.14 us
  transfers between devices with their start and end apart: 15, of which 10 were waited for; matrix products, arithmetic and copies ran while one was open for 11% of the time, Pallas kernels for 0%

profile of v5, /device:TPU:2, one launch (start us, length us, event | category | flops | bytes accessed | tf_op | source)
XLA Modules:
  0.0 138.8 jit_solution(4362578744116913136)
XLA Ops:
  2.6 3.5 %collective-permute-start.10 = (bf16[4096,128]{1,0:T(8,128)(2,1)}, bf16[4096,128]{1,0:T(8,128)(2,1)}, u32[]{:S(2)}, u32[]{:S(2)}) collective-permute-start(bf16[4096,128]{1,0:T(8,128)(2,1)} %dynamic-slice_bitcast_fusion), channel_id=1, source_target_pairs={{0,1},{1,0},{2,3},{3,2},{4,5},{5,4},{6,7},{7,6},{8,9},{9,8},{10,11... | collective-permute-start | bytes 3145736 | tf_op jit(solution)/shard_map/ppermute | solution.py:59
  7.4 6.2 %all-to-all-start = ((bf16[8,8,4096]{2,1,0:T(8,128)(2,1)}), bf16[8,8,4096]{2,1,0:T(8,128)(2,1)S(1)}, u32[]{:S(2)}, u32[]{:S(2)}) async-start(bf16[8,8,4096]{2,1,0:T(8,128)(2,1)} %bitcast.12), calls=%async_computation | async-start | bytes 1048576 | tf_op jit(solution)/shard_map/all_to_all | solution.py:47
  17.3 11.6 %all-to-all-done = bf16[8,8,4096]{2,1,0:T(8,128)(2,1)S(1)} async-done(((bf16[8,8,4096]{2,1,0:T(8,128)(2,1)}), bf16[8,8,4096]{2,1,0:T(8,128)(2,1)S(1)}, u32[]{:S(2)}, u32[]{:S(2)}) %all-to-all-start) | async-done | bytes 524320 | tf_op jit(solution)/shard_map/all_to_all | solution.py:47
  28.9 10.9 %collective-permute-start.2 = (bf16[64,4096]{1,0:T(8,128)(2,1)S(1)}, bf16[64,4096]{1,0:T(8,128)(2,1)S(1)}, u32[]{:S(2)}, u32[]{:S(2)}) collective-permute-start(bf16[64,4096]{1,0:T(8,128)(2,1)S(1)} %bitcast.149), channel_id=1, source_target_pairs={{0,56},{8,0},{16,8},{24,16},{32,24},{40,32},{48,40},{56,48},{1,57}... | collective-permute-start | bytes 1572872 | tf_op jit(solution)/shard_map/ppermute | solution.py:54
  39.9 1.9 %collective-permute-start.1 = (bf16[64,4096]{1,0:T(8,128)(2,1)S(1)}, bf16[64,4096]{1,0:T(8,128)(2,1)S(1)}, u32[]{:S(2)}, u32[]{:S(2)}) collective-permute-start(bf16[64,4096]{1,0:T(8,128)(2,1)S(1)} %bitcast.150), channel_id=1, source_target_pairs={{0,8},{8,16},{16,24},{24,32},{32,40},{40,48},{48,56},{56,0},{1,9},... | collective-permute-start | bytes 1572872 | tf_op jit(solution)/shard_map/ppermute | solution.py:54
  41.8 1.8 %pad_maximum_fusion = bf16[4096,256]{1,0:T(8,128)(2,1)S(1)} fusion(bf16[4096,128]{1,0:T(8,128)(2,1)} %collective-permute-done.10, bf16[4096,128]{1,0:T(8,128)(2,1)} %constant_dynamic-slice_fusion), kind=kLoop, calls=%fused_computation.17 | loop fusion | flops 4194304 | bytes 4194304 | tf_op jit(solution)/shard_map/concatenate | solution.py:141
  44.3 2.2 %collective-permute-done.2 = bf16[64,4096]{1,0:T(8,128)(2,1)S(1)} collective-permute-done((bf16[64,4096]{1,0:T(8,128)(2,1)S(1)}, bf16[64,4096]{1,0:T(8,128)(2,1)S(1)}, u32[]{:S(2)}, u32[]{:S(2)}) %collective-permute-start.2) | collective-permute-done | bytes 524320 | tf_op jit(solution)/shard_map/ppermute | solution.py:54
  46.5 5.6 %collective-permute-start.4 = (bf16[64,4096]{1,0:T(8,128)(2,1)S(1)}, bf16[64,4096]{1,0:T(8,128)(2,1)S(1)}, u32[]{:S(2)}, u32[]{:S(2)}) collective-permute-start(bf16[64,4096]{1,0:T(8,128)(2,1)S(1)} %collective-permute-done.2), channel_id=1, source_target_pairs={{0,56},{8,0},{16,8},{24,16},{32,24},{40,32},{48,40},{56,48},{1,57}... | collective-permute-start | bytes 1572872 | tf_op jit(solution)/shard_map/ppermute | solution.py:54
  52.1 1.9 %collective-permute-start.3 = (bf16[64,4096]{1,0:T(8,128)(2,1)S(1)}, bf16[64,4096]{1,0:T(8,128)(2,1)S(1)}, u32[]{:S(2)}, u32[]{:S(2)}) collective-permute-start(bf16[64,4096]{1,0:T(8,128)(2,1)S(1)} %collective-permute-done.1), channel_id=1, source_target_pairs={{0,8},{8,16},{16,24},{24,32},{32,40},{40,48},{48,56},{56,0},{1,9},... | collective-permute-start | bytes 1572872 | tf_op jit(solution)/shard_map/ppermute | solution.py:54
  55.1 3.7 %collective-permute-done.4 = bf16[64,4096]{1,0:T(8,128)(2,1)S(1)} collective-permute-done((bf16[64,4096]{1,0:T(8,128)(2,1)S(1)}, bf16[64,4096]{1,0:T(8,128)(2,1)S(1)}, u32[]{:S(2)}, u32[]{:S(2)}) %collective-permute-start.4) | collective-permute-done | bytes 524320 | tf_op jit(solution)/shard_map/ppermute | solution.py:54
  58.8 3.8 %collective-permute-start.8 = (bf16[64,2048]{1,0:T(8,128)(2,1)S(1)}, bf16[64,2048]{1,0:T(8,128)(2,1)S(1)}, u32[]{:S(2)}, u32[]{:S(2)}) collective-permute-start(bf16[64,2048]{1,0:T(8,128)(2,1)S(1)} %slice.109), channel_id=1, source_target_pairs={{0,48},{8,56},{16,0},{24,8},{32,16},{40,24},{48,32},{56,40},{1,49}... | collective-permute-start | bytes 786440 | tf_op jit(solution)/shard_map/ppermute | solution.py:54
  62.7 1.7 %collective-permute-done.3 = bf16[64,4096]{1,0:T(8,128)(2,1)S(1)} collective-permute-done((bf16[64,4096]{1,0:T(8,128)(2,1)S(1)}, bf16[64,4096]{1,0:T(8,128)(2,1)S(1)}, u32[]{:S(2)}, u32[]{:S(2)}) %collective-permute-start.3) | collective-permute-done | bytes 524320 | tf_op jit(solution)/shard_map/ppermute | solution.py:54
  64.5 1.9 %collective-permute-start.7 = (bf16[64,2048]{1,0:T(8,128)(2,1)S(1)}, bf16[64,2048]{1,0:T(8,128)(2,1)S(1)}, u32[]{:S(2)}, u32[]{:S(2)}) collective-permute-start(bf16[64,2048]{1,0:T(8,128)(2,1)S(1)} %slice.108), channel_id=1, source_target_pairs={{0,16},{8,24},{16,32},{24,40},{32,48},{40,56},{48,0},{56,8},{1,17}... | collective-permute-start | bytes 786440 | tf_op jit(solution)/shard_map/ppermute | solution.py:54
  66.4 6.1 %collective-permute-start.6 = (bf16[64,4096]{1,0:T(8,128)(2,1)S(1)}, bf16[64,4096]{1,0:T(8,128)(2,1)S(1)}, u32[]{:S(2)}, u32[]{:S(2)}) collective-permute-start(bf16[64,4096]{1,0:T(8,128)(2,1)S(1)} %collective-permute-done.4), channel_id=1, source_target_pairs={{0,56},{8,0},{16,8},{24,16},{32,24},{40,32},{48,40},{56,48},{1,57}... | collective-permute-start | bytes 1572872 | tf_op jit(solution)/shard_map/ppermute | solution.py:54
  72.5 1.9 %collective-permute-start.5 = (bf16[64,4096]{1,0:T(8,128)(2,1)S(1)}, bf16[64,4096]{1,0:T(8,128)(2,1)S(1)}, u32[]{:S(2)}, u32[]{:S(2)}) collective-permute-start(bf16[64,4096]{1,0:T(8,128)(2,1)S(1)} %collective-permute-done.3), channel_id=1, source_target_pairs={{0,8},{8,16},{16,24},{24,32},{32,40},{40,48},{48,56},{56,0},{1,9},... | collective-permute-start | bytes 1572872 | tf_op jit(solution)/shard_map/ppermute | solution.py:54
  79.4 5.3 %collective-permute-done.5 = bf16[64,4096]{1,0:T(8,128)(2,1)S(1)} collective-permute-done((bf16[64,4096]{1,0:T(8,128)(2,1)S(1)}, bf16[64,4096]{1,0:T(8,128)(2,1)S(1)}, u32[]{:S(2)}, u32[]{:S(2)}) %collective-permute-start.5) | collective-permute-done | bytes 524320 | tf_op jit(solution)/shard_map/ppermute | solution.py:54
  85.2 2.6 %collective-permute-start.9 = (bf16[32,4096]{1,0:T(8,128)(2,1)S(1)}, bf16[32,4096]{1,0:T(8,128)(2,1)S(1)}, u32[]{:S(2)}, u32[]{:S(2)}) collective-permute-start(bf16[32,4096]{1,0:T(8,128)(2,1)S(1)} %get-tuple-element.16), channel_id=1, source_target_pairs={{0,1},{1,0},{2,3},{3,2},{4,5},{5,4},{6,7},{7,6},{8,9},{9,8},{10,11... | collective-permute-start | bytes 786440 | tf_op jit(solution)/shard_map/ppermute | solution.py:59
  90.0 3.4 %collective-permute-done.9.theirs_ref = bf16[32,4096]{1,0:T(8,128)(2,1)S(1)} collective-permute-done((bf16[32,4096]{1,0:T(8,128)(2,1)S(1)}, bf16[32,4096]{1,0:T(8,128)(2,1)S(1)}, u32[]{:S(2)}, u32[]{:S(2)}) %collective-permute-start.9) | collective-permute-done | bytes 262176 | tf_op jit(solution)/shard_map/ppermute | solution.py:59
  94.6 6.1 %all-to-all-start.1 = ((bf16[64,16,128]{2,1,0:T(8,128)(2,1)}), bf16[64,16,128]{2,1,0:T(8,128)(2,1)S(1)}, u32[]{:S(2)}, u32[]{:S(2)}) async-start(bf16[64,16,128]{2,1,0:T(8,128)(2,1)} %shard_map.82), calls=%async_computation.1 | async-start | bytes 524288 | tf_op jit(solution)/shard_map/all_to_all | solution.py:203
  100.9 3.5 %collective-permute-start.11 = (f32[512,128]{1,0:T(8,128)S(1)}, f32[512,128]{1,0:T(8,128)S(1)}, u32[]{:S(2)}, u32[]{:S(2)}) collective-permute-start(f32[512,128]{1,0:T(8,128)S(1)} %bitcast.159), channel_id=1, source_target_pairs={{0,1},{1,0},{2,3},{3,2},{4,5},{5,4},{6,7},{7,6},{8,9},{9,8},{10,11... | collective-permute-start | bytes 786440 | tf_op jit(solution)/shard_map/ppermute | solution.py:59
  104.5 9.9 %all-to-all-done.1 = bf16[64,16,128]{2,1,0:T(8,128)(2,1)S(1)} async-done(((bf16[64,16,128]{2,1,0:T(8,128)(2,1)}), bf16[64,16,128]{2,1,0:T(8,128)(2,1)S(1)}, u32[]{:S(2)}, u32[]{:S(2)}) %all-to-all-start.1) | async-done | bytes 262176 | tf_op jit(solution)/shard_map/all_to_all | solution.py:203
  116.3 2.0 %fusion.33 = bf16[64,8,128]{2,1,0:T(8,128)(2,1)} fusion(bf16[512,4096]{0,1:T(8,128)(2,1)S(1)} %bitcast.148, bf16[4096,128]{1,0:T(8,128)(2,1)S(1)} %bitcast.156, f32[512,128]{1,0:T(8,128)S(1)} %collective-permute-done.11, f32[8,8,8,128]{3,2,1,0:T(8,128)S(1)} %bitcast_select_fusion.1), kind=kOutput, calls=%fused_computation.70 | convolution fusion | flops 537133056 | bytes 5898240 | tf_op jit(solution)/shard_map/dot_general | solution.py:219
  118.2 5.6 %all-to-all-start.2 = ((bf16[64,8,128]{2,1,0:T(8,128)(2,1)}), bf16[64,8,128]{2,1,0:T(8,128)(2,1)S(1)}, u32[]{:S(2)}, u32[]{:S(2)}) async-start(bf16[64,8,128]{2,1,0:T(8,128)(2,1)} %fusion.33), calls=%async_computation.2 | async-start | bytes 262144 | tf_op jit(solution)/shard_map/all_to_all | solution.py:225
  124.9 11.7 %all-to-all-done.2 = bf16[64,8,128]{2,1,0:T(8,128)(2,1)S(1)} async-done(((bf16[64,8,128]{2,1,0:T(8,128)(2,1)}), bf16[64,8,128]{2,1,0:T(8,128)(2,1)S(1)}, u32[]{:S(2)}, u32[]{:S(2)}) %all-to-all-start.2) | async-done | bytes 131104 | tf_op jit(solution)/shard_map/all_to_all | solution.py:225
  (88 shorter events, 23.2 us)
Async XLA Ops:
  0.0 1.6 %copy-start = (bf16[1,8192,128]{2,1,0:T(8,128)(2,1)S(1)}, bf16[1,8192,128]{2,1,0:T(8,128)(2,1)}, u32[]{:S(2)}) copy-start(bf16[1,8192,128]{2,1,0:T(8,128)(2,1)} %param.12) | copy-start | bytes 6291460
  0.0 6.4 %copy-start.5 = (f32[1,8192]{1,0:T(1,128)S(1)}, f32[1,8192]{1,0:T(1,128)}, u32[]{:S(2)}) copy-start(f32[1,8192]{1,0:T(1,128)} %param.11) | copy-start | bytes 98308
  0.0 6.3 %collective-permute-start = (bf16[8,8192]{1,0:T(8,128)(2,1)}, bf16[8,8192]{1,0:T(8,128)(2,1)S(1)}, u32[]{:S(2)}, u32[]{:S(2)}) collective-permute-start(bf16[8,8192]{1,0:T(8,128)(2,1)} %param.10), channel_id=1, source_target_pairs={{0,64},{64,128},{128,192},{192,256},{256,320},{320,384},{384,448},... | collective-permute-start | bytes 393224 | tf_op jit(solution)/shard_map/ppermute | solution.py:37
  1.6 12.0 %copy-start.4 = (s32[512]{0:T(512)S(1)}, s32[512]{0:T(512)}, u32[]{:S(2)}) copy-start(s32[512]{0:T(512)} %param.15) | copy-start | bytes 6148
  2.6 39.2 %collective-permute-start.10 = (bf16[4096,128]{1,0:T(8,128)(2,1)}, bf16[4096,128]{1,0:T(8,128)(2,1)}, u32[]{:S(2)}, u32[]{:S(2)}) collective-permute-start(bf16[4096,128]{1,0:T(8,128)(2,1)} %dynamic-slice_bitcast_fusion), channel_id=1, source_target_pairs={{0,1},{1,0},{2,3},{3,2},{4,5},{5,4},{6,7},{7,6},{8,9},{9,8},{10,11... | collective-permute-start | bytes 3145736 | tf_op jit(solution)/shard_map/ppermute | solution.py:59
  7.4 21.5 %all-to-all-start = ((bf16[8,8,4096]{2,1,0:T(8,128)(2,1)}), bf16[8,8,4096]{2,1,0:T(8,128)(2,1)S(1)}, u32[]{:S(2)}, u32[]{:S(2)}) async-start(bf16[8,8,4096]{2,1,0:T(8,128)(2,1)} %bitcast.12), calls=%async_computation | async-start | bytes 1048576 | tf_op jit(solution)/shard_map/all_to_all | solution.py:47
  28.9 17.6 %collective-permute-start.2 = (bf16[64,4096]{1,0:T(8,128)(2,1)S(1)}, bf16[64,4096]{1,0:T(8,128)(2,1)S(1)}, u32[]{:S(2)}, u32[]{:S(2)}) collective-permute-start(bf16[64,4096]{1,0:T(8,128)(2,1)S(1)} %bitcast.149), channel_id=1, source_target_pairs={{0,56},{8,0},{16,8},{24,16},{32,24},{40,32},{48,40},{56,48},{1,57}... | collective-permute-start | bytes 1572872 | tf_op jit(solution)/shard_map/ppermute | solution.py:54
  39.9 12.3 %collective-permute-start.1 = (bf16[64,4096]{1,0:T(8,128)(2,1)S(1)}, bf16[64,4096]{1,0:T(8,128)(2,1)S(1)}, u32[]{:S(2)}, u32[]{:S(2)}) collective-permute-start(bf16[64,4096]{1,0:T(8,128)(2,1)S(1)} %bitcast.150), channel_id=1, source_target_pairs={{0,8},{8,16},{16,24},{24,32},{32,40},{40,48},{48,56},{56,0},{1,9},... | collective-permute-start | bytes 1572872 | tf_op jit(solution)/shard_map/ppermute | solution.py:54
  46.5 12.3 %collective-permute-start.4 = (bf16[64,4096]{1,0:T(8,128)(2,1)S(1)}, bf16[64,4096]{1,0:T(8,128)(2,1)S(1)}, u32[]{:S(2)}, u32[]{:S(2)}) collective-permute-start(bf16[64,4096]{1,0:T(8,128)(2,1)S(1)} %collective-permute-done.2), channel_id=1, source_target_pairs={{0,56},{8,0},{16,8},{24,16},{32,24},{40,32},{48,40},{56,48},{1,57}... | collective-permute-start | bytes 1572872 | tf_op jit(solution)/shard_map/ppermute | solution.py:54
  52.1 12.3 %collective-permute-start.3 = (bf16[64,4096]{1,0:T(8,128)(2,1)S(1)}, bf16[64,4096]{1,0:T(8,128)(2,1)S(1)}, u32[]{:S(2)}, u32[]{:S(2)}) collective-permute-start(bf16[64,4096]{1,0:T(8,128)(2,1)S(1)} %collective-permute-done.1), channel_id=1, source_target_pairs={{0,8},{8,16},{16,24},{24,32},{32,40},{40,48},{48,56},{56,0},{1,9},... | collective-permute-start | bytes 1572872 | tf_op jit(solution)/shard_map/ppermute | solution.py:54
  58.8 16.6 %collective-permute-start.8 = (bf16[64,2048]{1,0:T(8,128)(2,1)S(1)}, bf16[64,2048]{1,0:T(8,128)(2,1)S(1)}, u32[]{:S(2)}, u32[]{:S(2)}) collective-permute-start(bf16[64,2048]{1,0:T(8,128)(2,1)S(1)} %slice.109), channel_id=1, source_target_pairs={{0,48},{8,56},{16,0},{24,8},{32,16},{40,24},{48,32},{56,40},{1,49}... | collective-permute-start | bytes 786440 | tf_op jit(solution)/shard_map/ppermute | solution.py:54
  64.5 12.6 %collective-permute-start.7 = (bf16[64,2048]{1,0:T(8,128)(2,1)S(1)}, bf16[64,2048]{1,0:T(8,128)(2,1)S(1)}, u32[]{:S(2)}, u32[]{:S(2)}) collective-permute-start(bf16[64,2048]{1,0:T(8,128)(2,1)S(1)} %slice.108), channel_id=1, source_target_pairs={{0,16},{8,24},{16,32},{24,40},{32,48},{40,56},{48,0},{56,8},{1,17}... | collective-permute-start | bytes 786440 | tf_op jit(solution)/shard_map/ppermute | solution.py:54
  66.4 12.7 %collective-permute-start.6 = (bf16[64,4096]{1,0:T(8,128)(2,1)S(1)}, bf16[64,4096]{1,0:T(8,128)(2,1)S(1)}, u32[]{:S(2)}, u32[]{:S(2)}) collective-permute-start(bf16[64,4096]{1,0:T(8,128)(2,1)S(1)} %collective-permute-done.4), channel_id=1, source_target_pairs={{0,56},{8,0},{16,8},{24,16},{32,24},{40,32},{48,40},{56,48},{1,57}... | collective-permute-start | bytes 1572872 | tf_op jit(solution)/shard_map/ppermute | solution.py:54
  72.5 12.3 %collective-permute-start.5 = (bf16[64,4096]{1,0:T(8,128)(2,1)S(1)}, bf16[64,4096]{1,0:T(8,128)(2,1)S(1)}, u32[]{:S(2)}, u32[]{:S(2)}) collective-permute-start(bf16[64,4096]{1,0:T(8,128)(2,1)S(1)} %collective-permute-done.3), channel_id=1, source_target_pairs={{0,8},{8,16},{16,24},{24,32},{32,40},{40,48},{48,56},{56,0},{1,9},... | collective-permute-start | bytes 1572872 | tf_op jit(solution)/shard_map/ppermute | solution.py:54
  85.2 8.3 %collective-permute-start.9 = (bf16[32,4096]{1,0:T(8,128)(2,1)S(1)}, bf16[32,4096]{1,0:T(8,128)(2,1)S(1)}, u32[]{:S(2)}, u32[]{:S(2)}) collective-permute-start(bf16[32,4096]{1,0:T(8,128)(2,1)S(1)} %get-tuple-element.16), channel_id=1, source_target_pairs={{0,1},{1,0},{2,3},{3,2},{4,5},{5,4},{6,7},{7,6},{8,9},{9,8},{10,11... | collective-permute-start | bytes 786440 | tf_op jit(solution)/shard_map/ppermute | solution.py:59
  89.1 4.4 %copy-start.1 = (bf16[1,1,8192,64]{2,3,1,0:T(8,128)(2,1)S(1)}, bf16[1,1,8192,64]{2,3,1,0:T(8,128)(2,1)}, u32[]{:S(2)}) copy-start(bf16[1,1,8192,64]{2,3,1,0:T(8,128)(2,1)} %param.13) | copy-start | bytes 3145732
  94.6 19.7 %all-to-all-start.1 = ((bf16[64,16,128]{2,1,0:T(8,128)(2,1)}), bf16[64,16,128]{2,1,0:T(8,128)(2,1)S(1)}, u32[]{:S(2)}, u32[]{:S(2)}) async-start(bf16[64,16,128]{2,1,0:T(8,128)(2,1)} %shard_map.82), calls=%async_computation.1 | async-start | bytes 524288 | tf_op jit(solution)/shard_map/all_to_all | solution.py:203
  100.9 14.4 %collective-permute-start.11 = (f32[512,128]{1,0:T(8,128)S(1)}, f32[512,128]{1,0:T(8,128)S(1)}, u32[]{:S(2)}, u32[]{:S(2)}) collective-permute-start(f32[512,128]{1,0:T(8,128)S(1)} %bitcast.159), channel_id=1, source_target_pairs={{0,1},{1,0},{2,3},{3,2},{4,5},{5,4},{6,7},{7,6},{8,9},{9,8},{10,11... | collective-permute-start | bytes 786440 | tf_op jit(solution)/shard_map/ppermute | solution.py:59
  115.1 1.2 copy-start.2
  116.3 7.6 %copy-start.3 = (bf16[8,2,16,1024]{3,2,1,0:T(8,128)(2,1)S(1)}, bf16[8,2,16,1024]{3,2,1,0:T(8,128)(2,1)}, u32[]{:S(2)}) copy-start(bf16[8,2,16,1024]{3,2,1,0:T(8,128)(2,1)} %param.17) | copy-start | bytes 1572868
  118.2 18.3 %all-to-all-start.2 = ((bf16[64,8,128]{2,1,0:T(8,128)(2,1)}), bf16[64,8,128]{2,1,0:T(8,128)(2,1)S(1)}, u32[]{:S(2)}, u32[]{:S(2)}) async-start(bf16[64,8,128]{2,1,0:T(8,128)(2,1)} %fusion.33), calls=%async_computation.2 | async-start | bytes 262144 | tf_op jit(solution)/shard_map/all_to_all | solution.py:225
